TPU v7x, 32 devices: a whole 2x2x4 slice. The times are simulated.
32 devices in a mesh: group: 2 (over y), seq: 4 (over z), expert: 2 (over x), fsdp: 2 (over core).
Axes of the slice: x: 2, y: 2, z: 4, core: 2. Of those that a mesh axis runs over, the one named last changes fastest.
Arguments:
- queries: bfloat16 [4096, 3072], P(('group', 'seq'), ('expert', 'fsdp')), parts along dimension 0, may hold values from -1000 to 1000
- keys: bfloat16 [4096, 3072], P(('group', 'seq'), ('expert', 'fsdp')), parts along dimension 0, may hold values from -10 to 10
- values: bfloat16 [4096, 3072], P(('group', 'seq'), ('expert', 'fsdp')), parts along dimension 0, may hold values from -12 to 12
- tokens: bfloat16 [4096, 3072], P(('group', 'seq', 'expert', 'fsdp')), parts along dimension 0, may hold values from -200 to 200
- modulation: float32 [6, 3072], P('group'), parts along dimension 0, may hold values from -3 to 3
- out_weight: bfloat16 [3072, 3072], P(('expert', 'fsdp')), may hold values from -0.21875 to 0.21875
- fc_in: bfloat16 [8, 1536, 3072], P(('seq', 'expert'), 'fsdp'), may hold values from -0.109375 to 0.109375
- fc_out: bfloat16 [8, 1536, 3072], P(('seq', 'expert'), 'fsdp'), may hold values from -0.15625 to 0.15625
- expert_ids: int32 [4096, 2], P(('group', 'seq', 'expert', 'fsdp')), parts along dimension 0, may hold values from 0 to 7, all different within a row; in each aligned block of 128 rows (0 to 127, 128 to 255, ...) at most 64 rows name the same one
- gate_weights: float32 [4096, 2], P(('group', 'seq', 'expert', 'fsdp')), parts along dimension 0, may hold values from 0.1 to 1
Outputs:
- layer_out: bfloat16 [4096, 3072], P(('group', 'seq', 'expert', 'fsdp')), parts along dimension 0
There are 2 independent parts, one for each index of `group`. A program takes and returns all parts, laid end to end along the dimension named above; an argument that names none is the same for every part. Nothing has to cross between parts.
Inputs may be any that keep to these rules, and one draw needn't show every extreme that they name: `expert_ids`: in each aligned block of 128 tokens (the rows of one device) no expert is named by more than 64 tokens; a token's 2 experts differ.
All inputs are finite; a program needn't handle non-finite values.
Results may differ from a plain program's by a relative error of at most 0.014.
Values may be sent and summed in bfloat16 or wider, within the bound.
No kernel may reach another device: no remote copies, remote signals or barrier semaphores. Data moves between devices by JAX's collectives and lax.ppermute only.
A program may use at most 192 MiB of HBM per device.

v0:
```python
import math

import jax
import jax.numpy as jnp
from jax import lax
from jax.sharding import PartitionSpec as P

D = 3072
HEAD_DIM = 128
TOP = 2


EPSILON = 1e-06


def expert_block(slot_rows, weight_in, weight_out):
    hidden_act = jax.nn.gelu(
        jnp.einsum("sd,hd->sh", slot_rows, weight_in, preferred_element_type=jnp.float32),
        approximate=True,
    )
    return jnp.dot(hidden_act.astype(jnp.bfloat16), weight_out, preferred_element_type=jnp.float32)


def per_device(
    queries, keys, values, tokens, modulation, out_weight, fc_in, fc_out, expert_ids, gate_weights
):
    query_rows, features = queries.shape
    head_count = features // HEAD_DIM
    query_heads = queries.reshape(query_rows, head_count, HEAD_DIM)
    score_scale = 1.0 / math.sqrt(HEAD_DIM)
    run_max = jnp.full((query_rows, head_count), -jnp.inf, jnp.float32)
    run_total = jnp.zeros((query_rows, head_count), jnp.float32)
    weighted = jnp.zeros((query_rows, head_count, HEAD_DIM), jnp.float32)
    key_piece = lax.all_gather(keys, "seq", axis=0, tiled=True)
    value_piece = lax.all_gather(values, "seq", axis=0, tiled=True)
    piece_rows = key_piece.shape[0]
    key_heads = key_piece.reshape(piece_rows, head_count, HEAD_DIM)
    value_heads = value_piece.reshape(piece_rows, head_count, HEAD_DIM)
    scores = (
        jnp.einsum("qhd,khd->qhk", query_heads, key_heads, preferred_element_type=jnp.float32)
        * score_scale
    )
    new_max = jnp.max(scores, axis=-1)
    factor = jnp.exp(run_max - new_max)
    exp_scores = jnp.exp(scores - new_max[:, :, None])
    run_total = run_total * factor + jnp.sum(exp_scores, axis=-1)
    weighted = weighted * factor[:, :, None] + jnp.einsum(
        "qhk,khd->qhd",
        exp_scores.astype(jnp.bfloat16),
        value_heads,
        preferred_element_type=jnp.float32,
    )
    run_max, run_total, weighted = (new_max, run_total, weighted)
    attended = (weighted / run_total[:, :, None]).reshape(query_rows, features).astype(jnp.bfloat16)
    token_rows = tokens.shape[0]
    projected = lax.psum_scatter(
        jnp.dot(attended, out_weight, preferred_element_type=jnp.float32).astype(jnp.bfloat16),
        ("expert", "fsdp"),
        scatter_dimension=0,
        tiled=True,
    ).astype(jnp.float32)
    residual = (tokens.astype(jnp.float32) + projected).astype(jnp.bfloat16)
    resid_full = residual.astype(jnp.float32)
    center = jnp.mean(resid_full, axis=1, keepdims=True)
    spread = jnp.mean((resid_full - center) ** 2, axis=1, keepdims=True)
    normed = (resid_full - center) * lax.rsqrt(spread + EPSILON) * (
        1.0 + modulation[1]
    ) + modulation[0]
    normed = normed.astype(jnp.bfloat16)
    experts_total = fc_in.shape[0] * lax.axis_size(("seq", "expert"))
    capacity = max(2, 2 * TOP * token_rows // experts_total)
    flat_ids = expert_ids.reshape(-1)
    onehot_ids = (flat_ids[:, None] == jnp.arange(experts_total, dtype=jnp.int32)[None, :]).astype(
        jnp.int32
    )
    earlier = jnp.cumsum(onehot_ids, axis=0) - onehot_ids
    slot_ids = jnp.sum(earlier * onehot_ids, axis=1)
    target = flat_ids * capacity + slot_ids
    repeated = jnp.repeat(normed, TOP, axis=0)
    outgoing = jnp.zeros((experts_total * capacity, D), jnp.bfloat16).at[target].set(repeated)
    outgoing = outgoing.reshape(experts_total, capacity, D)
    incoming = lax.all_to_all(outgoing, ("seq", "expert"), split_axis=0, concat_axis=0, tiled=True)
    flat_incoming = incoming.reshape(experts_total * capacity, D)
    expert_sum = expert_block(
        flat_incoming,
        lax.all_gather(fc_in, "fsdp", axis=1, tiled=True)[0],
        lax.all_gather(fc_out, "fsdp", axis=1, tiled=True)[0],
    )
    results = expert_sum.astype(jnp.bfloat16).reshape(experts_total, capacity, D)
    returned = lax.all_to_all(
        results, ("seq", "expert"), split_axis=0, concat_axis=0, tiled=True
    ).reshape(experts_total * capacity, D)
    picked = returned[target].astype(jnp.float32).reshape(token_rows, TOP, D)
    mixture = jnp.sum(picked * gate_weights[:, :, None], axis=1)
    return (resid_full + modulation[2] * mixture).astype(jnp.bfloat16)


def solution(mesh):
    placed = (
        P(("group", "seq"), ("expert", "fsdp")),
        P(("group", "seq"), ("expert", "fsdp")),
        P(("group", "seq"), ("expert", "fsdp")),
        P(("group", "seq", "expert", "fsdp"), None),
        P("group", None),
        P(("expert", "fsdp"), None),
        P(("seq", "expert"), "fsdp", None),
        P(("seq", "expert"), "fsdp", None),
        P(("group", "seq", "expert", "fsdp"), None),
        P(("group", "seq", "expert", "fsdp"), None),
    )
    return jax.shard_map(
        per_device,
        mesh=mesh,
        in_specs=placed,
        out_specs=P(("group", "seq", "expert", "fsdp"), None),
        check_vma=False,
    )
```

profile of v0, /device:TPU:0, one launch (start us, length us, event | category | flops | bytes accessed | tf_op | source)
XLA Modules:
  0.0 393.2 jit_solution(7721474299566544136)
XLA Ops:
  7.4 2.4 copy.15
  9.8 0.7 all-gather.7.cloned.1.call-update
  10.6 0.3 copy.16
  10.9 65.2 %all-gather.5.cloned.1.call-done = bf16[2048,768]{0,1:T(8,128)(2,1)} async-done(((bf16[512,768]{0,1:T(8,128)(2,1)}), bf16[2048,768]{0,1:T(8,128)(2,1)}) %all-gather.5.cloned.1.call-update) | async-done | bytes 3145744 | tf_op jit(solution)/shard_map/all_gather | solution.py:34
  76.1 12.5 %bitcast_reduce_fusion = (f32[512,6]{0,1:T(8,128)S(1)}, f32[6,2048,512]{2,1,0:T(8,128)}) fusion(bf16[2048,6,128]{0,2,1:T(8,128)(2,1)} %bitcast.60, bf16[512,6,128]{0,2,1:T(8,128)(2,1)S(1)} %bitcast.61), kind=kOutput, calls=%fused_computation.3 | convolution fusion | flops 1623192576 | bytes 29110272 | tf_op jit(solution)/shard_map/qhd,khd->qhk/dot_general | solution.py:40
  88.6 10.6 %fusion.1 = f32[512,6]{0,1:T(8,128)S(1)} fusion(f32[6,2048,512]{2,1,0:T(8,128)} %get-tuple-element.13, f32[512,6]{0,1:T(8,128)S(1)} %get-tuple-element.12), kind=kLoop, calls=%fused_computation.5 | loop fusion | flops 18871296 | bytes 25190400 | tf_op jit(solution)/shard_map/reduce_sum | solution.py:46
  99.2 40.5 %all-gather.7.cloned.1.call-done = bf16[2048,768]{1,0:T(8,128)(2,1)} async-done(((bf16[512,768]{1,0:T(8,128)(2,1)}), bf16[2048,768]{1,0:T(8,128)(2,1)}) %all-gather.7.cloned.1.call-update) | async-done | bytes 3145744 | tf_op jit(solution)/shard_map/all_gather | solution.py:35
  139.8 3.2 copy.19
  143.0 10.6 %fusion.34 = bf16[512,6,128]{0,2,1:T(8,128)(2,1)S(1)} fusion(bf16[2048,6,128]{0,2,1:T(8,128)(2,1)S(1)} %bitcast.64, f32[6,2048,512]{2,1,0:T(8,128)} %get-tuple-element.13, f32[512,6]{0,1:T(8,128)S(1)} %get-tuple-element.12, f32[512,6]{0,1:T(8,128)S(1)} %get-tuple-element.11, f32[512,6]{0,1:T(8,128)S(1)} %get-tuple-element.10), kind=kOutput, calls=%fused_computation.38 | convolution fusion | flops 1630666752 | bytes 29134848 | tf_op jit(solution)/shard_map/qhk,khd->qhd/dot_general | solution.py:47
  153.5 6.4 %convolution_convert_fusion = bf16[512,3072]{1,0:T(8,128)(2,1)} fusion(bf16[512,768]{0,1:T(8,128)(2,1)S(1)} %bitcast.71, bf16[768,3072]{1,0:T(8,128)(2,1)} %param.15), kind=kOutput, calls=%fused_computation.15 | convolution fusion | flops 2417491968 | bytes 8650752 | tf_op jit(solution)/shard_map/dot_general | solution.py:57
  160.0 0.5 all-gather.11.cloned.1.call-update
  160.6 0.2 all-gather.9.cloned.1.call-start
  160.8 0.4 all-gather.9.cloned.1.call-update
  161.6 0.6 reduce-window.6
  162.2 0.2 slice_reduce_fusion
  162.9 33.7 %reduce-scatter.2.cloned.1.call-done = bf16[128,3072]{1,0:T(8,128)(2,1)} async-done(((bf16[512,3072]{1,0:T(8,128)(2,1)}), bf16[128,3072]{1,0:T(8,128)(2,1)}) %reduce-scatter.2.cloned.1.call-update) | async-done | bytes 786448 | tf_op jit(solution)/shard_map/reduce_scatter | solution.py:56
  196.6 1.6 convert_reduce_fusion
  198.2 0.4 fusion.28
  198.6 0.5 copy-done
  199.1 0.4 fusion.31
  199.5 0.8 broadcast_in_dim.11
  200.3 0.6 reshape.122
  200.9 4.9 %scatter_custom_fusion = bf16[512,3072]{1,0:T(8,128)(2,1)} fusion(s32[256]{0:T(256)S(1)} %bitcast.68, bf16[256,3072]{1,0:T(8,128)(2,1)S(1)} %reshape.122, bf16[]{:T(256)} %constant.16.clone.1), kind=kCustom, calls=%fused_computation.39 | custom fusion | bytes 3145730 | tf_op jit(solution)/shard_map/scatter | solution.py:80
  205.8 4.7 %all-to-all-start = ((bf16[8,64,3072]{2,1,0:T(8,128)(2,1)}), bf16[8,64,3072]{2,1,0:T(8,128)(2,1)S(1)}, u32[]{:S(2)}, u32[]{:S(2)}) async-start(bf16[8,64,3072]{2,1,0:T(8,128)(2,1)} %bitcast.13), calls=%async_computation.1 | async-start | bytes 6291456 | tf_op jit(solution)/shard_map/all_to_all | solution.py:82
  210.6 70.5 %all-to-all-done = bf16[8,64,3072]{2,1,0:T(8,128)(2,1)S(1)} async-done(((bf16[8,64,3072]{2,1,0:T(8,128)(2,1)}), bf16[8,64,3072]{2,1,0:T(8,128)(2,1)S(1)}, u32[]{:S(2)}, u32[]{:S(2)}) %all-to-all-start) | async-done | bytes 3145760 | tf_op jit(solution)/shard_map/all_to_all | solution.py:82
  281.1 18.4 %fusion.11 = bf16[512,3072]{1,0:T(8,128)(2,1)} fusion(bf16[1,1536,3072]{2,1,0:T(8,128)(2,1)} %all-gather.11.cloned.1.call-done, bf16[512,3072]{1,0:T(8,128)(2,1)S(1)} %bitcast.62, bf16[1,1536,3072]{2,1,0:T(8,128)(2,1)} %all-gather.9.cloned.1.call-done), kind=kOutput, calls=%fused_computation.16 | convolution fusion | flops 9672327168 | bytes 25165824 | tf_op jit(solution)/shard_map/dot_general | solution.py:21
  299.5 4.0 %all-to-all-start.1 = ((bf16[8,64,3072]{2,1,0:T(8,128)(2,1)}), bf16[8,64,3072]{2,1,0:T(8,128)(2,1)S(1)}, u32[]{:S(2)}, u32[]{:S(2)}) async-start(bf16[8,64,3072]{2,1,0:T(8,128)(2,1)} %bitcast.63), calls=%async_computation.2 | async-start | bytes 6291456 | tf_op jit(solution)/shard_map/all_to_all | solution.py:90
  303.7 70.6 %all-to-all-done.1 = bf16[8,64,3072]{2,1,0:T(8,128)(2,1)S(1)} async-done(((bf16[8,64,3072]{2,1,0:T(8,128)(2,1)}), bf16[8,64,3072]{2,1,0:T(8,128)(2,1)S(1)}, u32[]{:S(2)}, u32[]{:S(2)}) %all-to-all-start.1) | async-done | bytes 3145760 | tf_op jit(solution)/shard_map/all_to_all | solution.py:90
  374.3 2.7 gather_fusion
  377.0 3.5 reshape.109
  380.5 4.5 %multiply_reduce_fusion = f32[128,3072]{1,0:T(8,128)S(1)} fusion(f32[128,2,3072]{2,1,0:T(2,128)S(1)} %reshape.109, f32[128,2]{1,0:T(8,128)S(1)} %copy.24), kind=kLoop, calls=%fused_computation.24 | loop fusion | flops 1179648 | bytes 4719616 | tf_op jit(solution)/shard_map/reduce_sum | solution.py:94
  385.0 1.1 fusion.32
  (38 shorter events, 1.3 us)
Async XLA Ops:
  7.4 3.2 copy-start.3
  7.4 68.7 %all-gather.5.cloned.1.call-start = ((), (), s32[]{:S(2)}) async-start(), calls=%async_computation.3 | async-start | bytes 3932160 | tf_op jit(solution)/shard_map/all_gather | solution.py:34
  9.8 130.0 %all-gather.7.cloned.1.call-start = ((), (), s32[]{:S(2)}) async-start(), calls=%async_computation.4 | async-start | bytes 3932160 | tf_op jit(solution)/shard_map/all_gather | solution.py:35
  10.5 186.1 %reduce-scatter.2.cloned.1.call-start = ((), (), s32[]{:S(2)}) async-start(), calls=%async_computation.5 | async-start | bytes 3932160 | tf_op jit(solution)/shard_map/reduce_scatter | solution.py:56
  159.9 50.6 %all-gather.11.cloned.1.call-start = ((), (), s32[]{:S(2)}) async-start(), calls=%async_computation.7 | async-start | bytes 14155776 | tf_op jit(solution)/shard_map/all_gather | solution.py:87
  160.5 0.7 copy-start.5
  160.5 2.3 copy-start.4
  160.5 36.1 %copy-start.2 = (bf16[128,3072]{1,0:T(8,128)(2,1)S(1)}, bf16[128,3072]{1,0:T(8,128)(2,1)}, u32[]{:S(2)}) copy-start(bf16[128,3072]{1,0:T(8,128)(2,1)} %param.13) | copy-start | bytes 2359300
  160.6 50.0 %all-gather.9.cloned.1.call-start = ((), (), s32[]{:S(2)}) async-start(), calls=%async_computation.6 | async-start | bytes 14155776 | tf_op jit(solution)/shard_map/all_gather | solution.py:86
  198.2 0.9 copy-start
  205.8 75.2 %all-to-all-start = ((bf16[8,64,3072]{2,1,0:T(8,128)(2,1)}), bf16[8,64,3072]{2,1,0:T(8,128)(2,1)S(1)}, u32[]{:S(2)}, u32[]{:S(2)}) async-start(bf16[8,64,3072]{2,1,0:T(8,128)(2,1)} %bitcast.13), calls=%async_computation.1 | async-start | bytes 6291456 | tf_op jit(solution)/shard_map/all_to_all | solution.py:82
  299.5 4.1 %copy-start.6 = (f32[128,2]{0,1:T(2,128)S(1)}, f32[128,2]{0,1:T(2,128)}, u32[]{:S(2)}) copy-start(f32[128,2]{0,1:T(2,128)} %param.19) | copy-start | bytes 3076
  299.5 74.8 %all-to-all-start.1 = ((bf16[8,64,3072]{2,1,0:T(8,128)(2,1)}), bf16[8,64,3072]{2,1,0:T(8,128)(2,1)S(1)}, u32[]{:S(2)}, u32[]{:S(2)}) async-start(bf16[8,64,3072]{2,1,0:T(8,128)(2,1)} %bitcast.63), calls=%async_computation.2 | async-start | bytes 6291456 | tf_op jit(solution)/shard_map/all_to_all | solution.py:90
  380.5 4.5 %copy-start.1 = (bf16[128,3072]{1,0:T(8,128)(2,1)S(1)}, bf16[128,3072]{1,0:T(8,128)(2,1)}, u32[]{:S(2)}) copy-start(bf16[128,3072]{1,0:T(8,128)(2,1)} %copy-done) | copy-start | bytes 2359300
Sparse Core Ops, SparseCore 0:
  9.9 66.1 all-gather.4
  77.6 62.0 all-gather.6
  160.1 36.5 reduce-scatter.1
Sparse Core Ops, SparseCore 1:
  162.0 20.2 all-gather.10
  183.6 22.6 all-gather.8
where the time goes:
time: 394 us; the launch traced here: 393 us
  waiting for transfers between devices  282 us (72%)
  matrix products  47.9 us (12%)
  local copies, waits for them, and re-layouts  20 us (5%)
  other arithmetic  19.3 us (5%)
  between operations  14.8 us (4%)
  starting transfers between devices  9.06 us (2%)
    all_to_all x1, waiting for transfers between devices, per_device(): lax.all_to_all(results, ('seq', 'expert'), split_axis=0, concat_axis=0, t...  70.6 us
    all_to_all x1, waiting for transfers between devices, per_device(): lax.all_to_all(outgoing, ('seq', 'expert'), split_axis=0, concat_axis=0,...  70.5 us
    all_gather x1, waiting for transfers between devices, per_device(): key_piece = lax.all_gather(keys, 'seq', axis=0, tiled=True)  65.2 us
    all_gather x1, waiting for transfers between devices, per_device(): value_piece = lax.all_gather(values, 'seq', axis=0, tiled=True)  40.5 us
    reduce_scatter x1, waiting for transfers between devices, per_device(): lax.psum_scatter(jnp.dot(attended, out_weight, preferred_element_type=jnp...  33.7 us
    dot_general x1, matrix products, expert_block(): jnp.dot(hidden_act.astype(jnp.bfloat16), weight_out, preferred_element_ty...  18.4 us
    dot_general x1, matrix products, per_device(): jnp.einsum('qhd,khd->qhk', query_heads, key_heads, preferred_element_type...  12.5 us
    reduce_sum x1, other arithmetic, per_device(): run_total = run_total * factor + jnp.sum(exp_scores, axis=-1)  10.6 us
  transfers between devices with their start and end apart: 7, of which 5 were waited for; matrix products, arithmetic and copies ran while one was open for 9% of the time, Pallas kernels for 0%

commit v1 on v0

v1 whole, which is shorter than its diff:
```python
import math
from functools import partial

import jax
import jax.numpy as jnp
from jax import lax
from jax.experimental import pallas as pl
from jax.experimental.pallas import tpu as pltpu
from jax.sharding import PartitionSpec as P

HEAD_DIM = 128
TOP = 2
EPSILON = 1e-06
LOG2E = 1.4426950408889634
VMEM_LIMIT = 60 * 1024 * 1024


def expert_block(slot_rows, weight_in, weight_out):
    hidden_act = jax.nn.gelu(
        jnp.einsum("sd,hd->sh", slot_rows, weight_in, preferred_element_type=jnp.float32),
        approximate=True,
    )
    return jnp.dot(hidden_act.astype(jnp.bfloat16), weight_out, preferred_element_type=jnp.float32)


def attend_tile(query, key_list, value_list):
    factor = LOG2E / math.sqrt(HEAD_DIM)
    scores = [
        lax.dot_general(query, k, (((1,), (1,)), ((), ())), preferred_element_type=jnp.float32)
        for k in key_list
    ]
    top = scores[0].max(axis=1, keepdims=True)
    for s in scores[1:]:
        top = jnp.maximum(top, s.max(axis=1, keepdims=True))
    total, mixed = 0.0, 0.0
    for s, v in zip(scores, value_list):
        p = jnp.exp2((s - top) * factor)
        total = total + p.sum(axis=1, keepdims=True)
        mixed = mixed + jnp.dot(p.astype(jnp.bfloat16), v, preferred_element_type=jnp.float32)
    return (mixed / total).astype(jnp.bfloat16)


def attention_kernel(parts, query_ref, *refs):
    out_ref = refs[-1]
    keys = [refs[2 * i][...].reshape(-1, HEAD_DIM) for i in range(parts)]
    values = [refs[2 * i + 1][...].reshape(-1, HEAD_DIM) for i in range(parts)]
    out_ref[...] = attend_tile(query_ref[0, 0], keys, values)


def attention(packs, tile):
    planes, _, rows, _ = packs[0].shape
    per = rows // tile
    specs = [pl.BlockSpec((1, 1, tile, HEAD_DIM), lambda i: (i // per, 0, i % per, 0))]
    operands = [packs[0]]
    for pack in packs:
        for which in (1, 2):
            specs.append(
                pl.BlockSpec(
                    (planes, 1, pack.shape[2], HEAD_DIM), lambda i, which=which: (0, which, 0, 0)
                )
            )
            operands.append(pack)
    all_keys = sum(p.shape[0] * p.shape[2] for p in packs)
    return pl.pallas_call(
        partial(attention_kernel, len(packs)),
        grid=(planes * per,),
        in_specs=specs,
        out_specs=pl.BlockSpec((tile, HEAD_DIM), lambda i: (i, 0)),
        out_shape=jax.ShapeDtypeStruct((planes * rows, HEAD_DIM), jnp.bfloat16),
        compiler_params=pltpu.CompilerParams(vmem_limit_bytes=VMEM_LIMIT),
        cost_estimate=pl.CostEstimate(
            flops=4 * planes * rows * all_keys * HEAD_DIM,
            transcendentals=planes * rows * all_keys,
            bytes_accessed=2 * HEAD_DIM * (2 * planes * rows + 2 * all_keys),
        ),
        name="attention",
    )(*operands)


def swap(axis):
    return partial(lax.ppermute, axis_name=axis, perm=[(0, 1), (1, 0)])


def project_kernel(counts, slots_ref, full_ref, shared_ref, tokens_ref, mod_ref, *refs):
    pieces = refs[: len(counts)]
    residual_ref, normed_ref, buf, acc, sems = refs[len(counts) :]
    copies, slot = [], 0
    for piece, count in zip(pieces, counts):
        for i in range(count):
            copies.append(
                pltpu.make_async_copy(
                    piece.at[pl.ds(i * HEAD_DIM, HEAD_DIM), :],
                    buf.at[pl.ds(slot * HEAD_DIM, HEAD_DIM), :],
                    sems.at[slot],
                )
            )
            slot += 1
    for copy in copies:
        copy.start()
    full_heads = full_ref.shape[0]

    def head(i):
        where = slots_ref[i]
        is_full = where < full_heads
        one = full_ref[jnp.minimum(where, full_heads - 1)]
        two = shared_ref[jnp.maximum(where - full_heads, 0)]
        return jnp.where(is_full, one, two)

    acc[...] = tokens_ref[...].astype(jnp.float32)
    for i in range(0, slot, 2):
        copies[i].wait()
        copies[i + 1].wait()
        left = jnp.concatenate([head(i), head(i + 1)], axis=1)
        acc[...] += jnp.dot(
            left, buf[pl.ds(i * HEAD_DIM, 2 * HEAD_DIM), :], preferred_element_type=jnp.float32
        )
    residual = acc[...].astype(jnp.bfloat16)
    residual_ref[...] = residual
    full = residual.astype(jnp.float32)
    center = jnp.mean(full, axis=1, keepdims=True)
    spread = jnp.mean((full - center) ** 2, axis=1, keepdims=True)
    normed = (full - center) * lax.rsqrt(spread + EPSILON) * (1.0 + mod_ref[1:2, :]) + mod_ref[0:1, :]
    normed_ref[...] = normed.astype(jnp.bfloat16)


def moved_heads_attention(queries, keys, values, tokens, modulation, out_weight):
    planes = lax.axis_size("seq")
    query_rows, features = queries.shape
    heads = features // HEAD_DIM
    blocks = lax.axis_size(("expert", "fsdp"))
    token_rows = tokens.shape[0]
    half = token_rows // 2
    mine = [t.reshape(query_rows, heads, HEAD_DIM) for t in (queries, keys, values)]

    first = jnp.stack([t[:, :planes].transpose(1, 0, 2) for t in mine], axis=1)
    other = jnp.stack(
        [
            t[:, planes:].reshape(blocks, 2, half, heads - planes, HEAD_DIM).transpose(1, 3, 0, 2, 4)
            for t in mine
        ],
        axis=2,
    ).reshape(2, heads - planes, 3, blocks * half, HEAD_DIM)
    first_in = lax.all_to_all(first, "seq", split_axis=0, concat_axis=0, tiled=True)
    core = lax.axis_index("fsdp")
    sent = lax.dynamic_index_in_dim(other, 1 - core, 0, keepdims=False)
    kept = lax.dynamic_index_in_dim(other, core, 0, keepdims=False)
    came = swap("fsdp")(sent)
    second = jnp.where(
        core == 0, jnp.concatenate([kept, came], 0), jnp.concatenate([came, kept], 0)
    )
    second_in = lax.all_to_all(second, "seq", split_axis=0, concat_axis=0, tiled=True)
    second_pair = swap("fsdp")(second_in)

    group = lax.axis_index("group")
    rows_half = (heads // 2) * HEAD_DIM
    to_x = lax.dynamic_slice_in_dim(out_weight, group * rows_half, rows_half, 0)
    pieces = [out_weight, swap("fsdp")(out_weight)]
    from_x, from_y = [], []
    for i in range(heads // 2):
        from_x.append(swap("expert")(to_x[i * HEAD_DIM : (i + 1) * HEAD_DIM]))
    for piece in from_x:
        from_y.append(swap("group")(piece))
    pieces += from_x + from_y
    pieces += [swap("fsdp")(p) for p in from_x + from_y]

    tile = min(256, query_rows)
    first_out = attention([first_in], tile)
    first_back = lax.all_to_all(
        first_out.reshape(planes * blocks, token_rows, HEAD_DIM),
        ("seq", "expert", "fsdp"),
        split_axis=0,
        concat_axis=0,
        tiled=True,
    )
    second_out = attention([second_in, second_pair], tile)
    second_back = lax.all_to_all(
        second_out.reshape(planes * blocks, half, HEAD_DIM),
        ("seq", "expert", "fsdp"),
        split_axis=0,
        concat_axis=0,
        tiled=True,
    ).reshape(planes * 2, token_rows, HEAD_DIM)

    col = lax.axis_index("expert")
    full_heads = planes * blocks

    def slots(x, c, which):
        return [
            p * blocks + 2 * x + c
            if p < planes
            else full_heads + (2 * c + p - planes) * 2 + x
            for p in which
        ]

    everything = jnp.arange(heads)

    def slot_of(x, c, p):
        return jnp.where(
            p < planes, p * blocks + 2 * x + c, full_heads + (2 * c + p - planes) * 2 + x
        )

    near = group * (heads // 2) + jnp.arange(heads // 2)
    far = (1 - group) * (heads // 2) + jnp.arange(heads // 2)
    table = jnp.concatenate(
        [
            slot_of(col, core, everything),
            slot_of(col, 1 - core, everything),
            slot_of(1 - col, core, near),
            slot_of(1 - col, core, far),
            slot_of(1 - col, 1 - core, near),
            slot_of(1 - col, 1 - core, far),
        ]
    ).astype(jnp.int32)
    counts = tuple(p.shape[0] // HEAD_DIM for p in pieces)
    width = out_weight.shape[1]
    total = sum(counts)
    vmem = pl.BlockSpec(memory_space=pltpu.VMEM)
    return pl.pallas_call(
        partial(project_kernel, counts),
        in_specs=[pl.BlockSpec(memory_space=pltpu.SMEM)]
        + [vmem] * 4
        + [pl.BlockSpec(memory_space=pl.ANY)] * len(pieces),
        out_specs=[vmem, vmem],
        out_shape=[jax.ShapeDtypeStruct((token_rows, width), jnp.bfloat16)] * 2,
        scratch_shapes=[
            pltpu.VMEM((total * HEAD_DIM, width), jnp.bfloat16),
            pltpu.VMEM((token_rows, width), jnp.float32),
            pltpu.SemaphoreType.DMA((total,)),
        ],
        compiler_params=pltpu.CompilerParams(vmem_limit_bytes=VMEM_LIMIT),
        cost_estimate=pl.CostEstimate(
            flops=2 * token_rows * total * HEAD_DIM * width,
            transcendentals=0,
            bytes_accessed=2 * total * HEAD_DIM * width,
        ),
        name="project",
    )(table, first_back, second_back, tokens, modulation, *pieces)


def gathered_attention(queries, keys, values, tokens, modulation, out_weight):
    query_rows, features = queries.shape
    head_count = features // HEAD_DIM
    query_heads = queries.reshape(query_rows, head_count, HEAD_DIM)
    key_piece = lax.all_gather(keys, "seq", axis=0, tiled=True)
    value_piece = lax.all_gather(values, "seq", axis=0, tiled=True)
    piece_rows = key_piece.shape[0]
    key_heads = key_piece.reshape(piece_rows, head_count, HEAD_DIM)
    value_heads = value_piece.reshape(piece_rows, head_count, HEAD_DIM)
    scores = jnp.einsum(
        "qhd,khd->qhk", query_heads, key_heads, preferred_element_type=jnp.float32
    ) * (1.0 / math.sqrt(HEAD_DIM))
    exp_scores = jnp.exp(scores - jnp.max(scores, axis=-1, keepdims=True))
    weighted = jnp.einsum(
        "qhk,khd->qhd",
        exp_scores.astype(jnp.bfloat16),
        value_heads,
        preferred_element_type=jnp.float32,
    )
    attended = weighted / jnp.sum(exp_scores, axis=-1)[:, :, None]
    attended = attended.reshape(query_rows, features).astype(jnp.bfloat16)
    projected = lax.psum_scatter(
        jnp.dot(attended, out_weight, preferred_element_type=jnp.float32).astype(jnp.bfloat16),
        ("expert", "fsdp"),
        scatter_dimension=0,
        tiled=True,
    ).astype(jnp.float32)
    residual = (tokens.astype(jnp.float32) + projected).astype(jnp.bfloat16)
    resid_full = residual.astype(jnp.float32)
    center = jnp.mean(resid_full, axis=1, keepdims=True)
    spread = jnp.mean((resid_full - center) ** 2, axis=1, keepdims=True)
    normed = (resid_full - center) * lax.rsqrt(spread + EPSILON) * (
        1.0 + modulation[1]
    ) + modulation[0]
    return residual, normed.astype(jnp.bfloat16)


def sent_tokens_experts(normed, fc_in, fc_out, expert_ids, gate_weights):
    token_rows, width = normed.shape
    experts_total = fc_in.shape[0] * lax.axis_size(("seq", "expert"))
    capacity = max(2, 2 * TOP * token_rows // experts_total)
    flat_ids = expert_ids.reshape(-1)
    onehot_ids = (flat_ids[:, None] == jnp.arange(experts_total, dtype=jnp.int32)[None, :]).astype(
        jnp.int32
    )
    earlier = jnp.cumsum(onehot_ids, axis=0) - onehot_ids
    slot_ids = jnp.sum(earlier * onehot_ids, axis=1)
    target = flat_ids * capacity + slot_ids
    repeated = jnp.repeat(normed, TOP, axis=0)
    outgoing = jnp.zeros((experts_total * capacity, width), jnp.bfloat16).at[target].set(repeated)
    outgoing = outgoing.reshape(experts_total, capacity, width)
    incoming = lax.all_to_all(outgoing, ("seq", "expert"), split_axis=0, concat_axis=0, tiled=True)
    flat_incoming = incoming.reshape(experts_total * capacity, width)
    expert_sum = expert_block(
        flat_incoming,
        lax.all_gather(fc_in, "fsdp", axis=1, tiled=True)[0],
        lax.all_gather(fc_out, "fsdp", axis=1, tiled=True)[0],
    )
    results = expert_sum.astype(jnp.bfloat16).reshape(experts_total, capacity, width)
    returned = lax.all_to_all(
        results, ("seq", "expert"), split_axis=0, concat_axis=0, tiled=True
    ).reshape(experts_total * capacity, width)
    picked = returned[target].astype(jnp.float32).reshape(token_rows, TOP, width)
    return jnp.sum(picked * gate_weights[:, :, None], axis=1)


def per_device(
    queries, keys, values, tokens, modulation, out_weight, fc_in, fc_out, expert_ids, gate_weights
):
    planes = lax.axis_size("seq")
    heads = queries.shape[1] // HEAD_DIM
    pairs = all(lax.axis_size(a) == 2 for a in ("group", "expert", "fsdp"))
    if pairs and heads % 2 == 0 and heads > planes and 2 * (heads - planes) == planes:
        residual, normed = moved_heads_attention(
            queries, keys, values, tokens, modulation, out_weight
        )
    else:
        residual, normed = gathered_attention(
            queries, keys, values, tokens, modulation, out_weight
        )
    mixture = sent_tokens_experts(normed, fc_in, fc_out, expert_ids, gate_weights)
    return (residual.astype(jnp.float32) + modulation[2] * mixture).astype(jnp.bfloat16)


def solution(mesh):
    placed = (
        P(("group", "seq"), ("expert", "fsdp")),
        P(("group", "seq"), ("expert", "fsdp")),
        P(("group", "seq"), ("expert", "fsdp")),
        P(("group", "seq", "expert", "fsdp"), None),
        P("group", None),
        P(("expert", "fsdp"), None),
        P(("seq", "expert"), "fsdp", None),
        P(("seq", "expert"), "fsdp", None),
        P(("group", "seq", "expert", "fsdp"), None),
        P(("group", "seq", "expert", "fsdp"), None),
    )
    return jax.shard_map(
        per_device,
        mesh=mesh,
        in_specs=placed,
        out_specs=P(("group", "seq", "expert", "fsdp"), None),
        check_vma=False,
    )
```

time: 394 us -> 353 us (0.90)
  waiting for transfers between devices: 282 us -> 218 us
  starting transfers between devices: 9.06 us -> 39.8 us
  matrix products: 47.9 us -> 18.4 us
  Pallas kernels: 0 us -> 26.7 us
  other arithmetic: 19.3 us -> 9.95 us
  local copies, waits for them, and re-layouts: 20 us -> 25.5 us
    all_gather x4 -> x2, waiting for transfers between devices: 106 us -> 0.03 us  [the longest x1 0.02 us: sent_tokens_experts(): lax.all_gather(fc_out, 'fsdp', axis=1, tiled=True)[0]]
    ppermute x0 -> x15, waiting for transfers between devices: none -> 50.7 us  [the longest x3 45.8 us: moved_heads_attention(): from_x.append(swap('expert')(to_x[i * HEAD_DIM:(i + 1) * HEAD_DIM]))]
    reduce_scatter x1 -> x0, waiting for transfers between devices: 33.7 us -> none  [per_device(): lax.psum_scatter(jnp.dot(attended, out_weight, preferred_element_type=jnp...]
    dot_general x3 -> x0, matrix products: 29.4 us -> none  [the longest x1 12.5 us: per_device(): jnp.einsum('qhd,khd->qhk', query_heads, key_heads, preferred_element_type...]
    pallas_call x0 -> x3, Pallas kernels: none -> 26.7 us  [the longest x2 16.9 us: attention(): pl.pallas_call(partial(attention_kernel, len(packs)), grid=(planes * per,...]
    all_to_all x2 -> x6, waiting for transfers between devices: 141 us -> 165 us  [the longest x1 71.2 us: sent_tokens_experts(): lax.all_to_all(outgoing, ('seq', 'expert'), split_axis=0, concat_axis=0,...]
    all_to_all x2 -> x6, starting transfers between devices: 8.71 us -> 29.7 us  [the longest x1 6.23 us: moved_heads_attention(): lax.all_to_all(second, 'seq', split_axis=0, concat_axis=0, tiled=True)]
    reduce_sum x5 -> x2, other arithmetic: 17.1 us -> 4.56 us  [the longest x1 4.47 us: sent_tokens_experts(): return jnp.sum(picked * gate_weights[:, :, None], axis=1)]
  transfers between devices with their start and end apart: 7 -> 23, of which waited for: 5 -> 11; matrix products, arithmetic and copies ran while one was open for 9% -> 6% of each run, Pallas kernels for 0% -> 8%
where the time goes in v1:
time: 353 us; the launch traced here: 352 us
  waiting for transfers between devices  218 us (62%)
  starting transfers between devices  39.8 us (11%)
  Pallas kernels  26.7 us (8%)
  local copies, waits for them, and re-layouts  25.5 us (7%)
  matrix products  18.4 us (5%)
  between operations  13.8 us (4%)
  other arithmetic  9.95 us (3%)
    all_to_all x1, waiting for transfers between devices, sent_tokens_experts(): lax.all_to_all(outgoing, ('seq', 'expert'), split_axis=0, concat_axis=0,...  71.2 us
    all_to_all x1, waiting for transfers between devices, sent_tokens_experts(): lax.all_to_all(results, ('seq', 'expert'), split_axis=0, concat_axis=0, t...  69.8 us
    ppermute x3, waiting for transfers between devices, moved_heads_attention(): from_x.append(swap('expert')(to_x[i * HEAD_DIM:(i + 1) * HEAD_DIM]))  45.8 us
    dot_general x1, matrix products, expert_block(): jnp.dot(hidden_act.astype(jnp.bfloat16), weight_out, preferred_element_ty...  18.4 us
    pallas_call x2, Pallas kernels, attention(): pl.pallas_call(partial(attention_kernel, len(packs)), grid=(planes * per,...  16.9 us
    all_to_all x1, waiting for transfers between devices, moved_heads_attention(): lax.all_to_all(second, 'seq', split_axis=0, concat_axis=0, tiled=True)  16.1 us
    pallas_call x1, Pallas kernels, moved_heads_attention(): pl.pallas_call(partial(project_kernel, counts), in_specs=[pl.BlockSpec(me...  9.81 us
    all_to_all x1, waiting for transfers between devices, moved_heads_attention(): lax.all_to_all(first_out.reshape(planes * blocks, token_rows, HEAD_DIM),...  8.32 us
  transfers between devices with their start and end apart: 23, of which 11 were waited for; matrix products, arithmetic and copies ran while one was open for 6% of the time, Pallas kernels for 8%

profile of v1, /device:TPU:0, one launch (start us, length us, event | category | flops | bytes accessed | tf_op | source)
XLA Modules:
  0.0 351.9 jit_solution(11447907111027124493)
XLA Ops:
  11.1 1.5 collective-permute-done
  12.6 2.1 maximum_select_fusion
  14.7 6.2 %all-to-all-start.2 = ((bf16[4,3,256,128]{3,2,1,0:T(8,128)(2,1)}), bf16[4,3,256,128]{3,2,1,0:T(8,128)(2,1)S(1)}, u32[]{:S(2)}, u32[]{:S(2)}) async-start(bf16[4,3,256,128]{3,2,1,0:T(8,128)(2,1)} %maximum_select_fusion), calls=%async_computation.2 | async-start | bytes 1572864 | tf_op jit(solution)/shard_map/all_to_all | solution.py:151
  21.8 1.4 copy.59
  23.8 1.4 pad_maximum_fusion
  25.2 16.1 %all-to-all-done.2.query_ref.refs_0_.refs_1_ = bf16[4,3,256,128]{3,2,1,0:T(8,128)(2,1)S(1)} async-done(((bf16[4,3,256,128]{3,2,1,0:T(8,128)(2,1)}), bf16[4,3,256,128]{3,2,1,0:T(8,128)(2,1)S(1)}, u32[]{:S(2)}, u32[]{:S(2)}) %all-to-all-start.2) | async-done | bytes 786464 | tf_op jit(solution)/shard_map/all_to_all | solution.py:151
  41.3 3.6 %all-to-all-start = ((bf16[4,3,512,128]{3,2,1,0:T(8,128)(2,1)}), bf16[4,3,512,128]{3,2,1,0:T(8,128)(2,1)S(1)}, u32[]{:S(2)}, u32[]{:S(2)}) async-start(bf16[4,3,512,128]{3,2,1,0:T(8,128)(2,1)} %pad_maximum_fusion), calls=%async_computation | async-start | bytes 3145728 | tf_op jit(solution)/shard_map/all_to_all | solution.py:143
  45.7 1.8 constant_dynamic-slice_fusion.2
  47.5 1.6 collective-permute-start.3
  49.6 1.5 collective-permute-start.5
  51.0 16.9 %collective-permute-done.3.refs_2_ = bf16[128,3072]{1,0:T(8,128)(2,1)S(1)} collective-permute-done((bf16[128,3072]{1,0:T(8,128)(2,1)S(1)}, bf16[128,3072]{1,0:T(8,128)(2,1)S(1)}, u32[]{:S(2)}, u32[]{:S(2)}) %collective-permute-start.3) | collective-permute-done | bytes 786464 | tf_op jit(solution)/shard_map/ppermute | solution.py:160
  67.9 1.5 collective-permute-start.6
  69.5 15.4 %collective-permute-done.4.refs_3_ = bf16[128,3072]{1,0:T(8,128)(2,1)} collective-permute-done((bf16[128,3072]{1,0:T(8,128)(2,1)S(1)}, bf16[128,3072]{1,0:T(8,128)(2,1)}, u32[]{:S(2)}, u32[]{:S(2)}) %collective-permute-start.4) | collective-permute-done | bytes 786464 | tf_op jit(solution)/shard_map/ppermute | solution.py:160
  84.9 1.5 collective-permute-start.7
  86.4 13.5 %collective-permute-done.5.refs_4_ = bf16[128,3072]{1,0:T(8,128)(2,1)} collective-permute-done((bf16[128,3072]{1,0:T(8,128)(2,1)S(1)}, bf16[128,3072]{1,0:T(8,128)(2,1)}, u32[]{:S(2)}, u32[]{:S(2)}) %collective-permute-start.5) | collective-permute-done | bytes 786464 | tf_op jit(solution)/shard_map/ppermute | solution.py:160
  99.9 1.6 collective-permute-start.8
  102.4 6.2 %attention.3 = bf16[1024,128]{1,0:T(8,128)(2,1)} custom-call(bf16[4,3,256,128]{3,2,1,0:T(8,128)(2,1)} %copy-done, bf16[4,3,256,128]{3,2,1,0:T(8,128)(2,1)} %copy-done, bf16[4,3,256,128]{3,2,1,0:T(8,128)(2,1)} %copy-done, bf16[4,3,256,128]{3,2,1,0:T(8,128)(2,1)} %copy-done.1, bf16[4,3,256,128]{3,2,1,0:T(8,128)(2,1)} %copy-done.1), custom_call_target="tpu_custom_call" | custom-call | flops 1073741824 | bytes 1572864 | tf_op jit(solution)/shard_map/attention/pallas_call | solution.py:64
  108.6 5.8 %all-to-all-start.3 = ((bf16[16,64,128]{2,1,0:T(8,128)(2,1)}), bf16[16,64,128]{2,1,0:T(8,128)(2,1)S(1)}, u32[]{:S(2)}, u32[]{:S(2)}) async-start(bf16[16,64,128]{2,1,0:T(8,128)(2,1)} %bitcast.77), calls=%async_computation.3 | async-start | bytes 524288 | tf_op jit(solution)/shard_map/all_to_all | solution.py:176
  115.4 10.7 %attention.2 = bf16[2048,128]{1,0:T(8,128)(2,1)} custom-call(bf16[4,3,512,128]{3,2,1,0:T(8,128)(2,1)} %copy-done.3, bf16[4,3,512,128]{3,2,1,0:T(8,128)(2,1)} %copy-done.3, bf16[4,3,512,128]{3,2,1,0:T(8,128)(2,1)} %copy-done.3), custom_call_target="tpu_custom_call" | custom-call | flops 2147483648 | bytes 2097152 | tf_op jit(solution)/shard_map/attention/pallas_call | solution.py:64
  126.2 6.0 %all-to-all-start.1 = ((bf16[16,128,128]{2,1,0:T(8,128)(2,1)}), bf16[16,128,128]{2,1,0:T(8,128)(2,1)S(1)}, u32[]{:S(2)}, u32[]{:S(2)}) async-start(bf16[16,128,128]{2,1,0:T(8,128)(2,1)} %bitcast.84), calls=%async_computation.1 | async-start | bytes 1048576 | tf_op jit(solution)/shard_map/all_to_all | solution.py:168
  138.1 8.3 %all-to-all-done.1.full_ref = bf16[16,128,128]{2,1,0:T(8,128)(2,1)S(1)} async-done(((bf16[16,128,128]{2,1,0:T(8,128)(2,1)}), bf16[16,128,128]{2,1,0:T(8,128)(2,1)S(1)}, u32[]{:S(2)}, u32[]{:S(2)}) %all-to-all-start.1) | async-done | bytes 524320 | tf_op jit(solution)/shard_map/all_to_all | solution.py:168
  147.3 9.8 %project.1 = (bf16[128,3072]{1,0:T(8,128)(2,1)}, bf16[128,3072]{1,0:T(8,128)(2,1)}) custom-call(s32[24]{0:T(128)} %concatenate.10.slots_ref, bf16[16,128,128]{2,1,0:T(8,128)(2,1)} %copy-done.2, bf16[8,128,128]{2,1,0:T(8,128)(2,1)} %bitcast.76, bf16[128,3072]{1,0:T(8,128)(2,1)} %tokens_ref.1, f32[3,3072]{1,0:T(4,128)} %mod_ref.1, bf16[768,3072]{1,0:T(8,128)(2,1)} %refs_0_.1, ...), custom_call_target="tpu_custom_call" | custom-call | flops 2415919104 | bytes 18874368 | tf_op jit(solution)/shard_map/project/pallas_call | solution.py:218
  157.1 1.9 broadcast_in_dim.5
  159.7 4.9 %scatter_custom_fusion = bf16[512,3072]{1,0:T(8,128)(2,1)} fusion(s32[256]{0:T(256)S(1)} %bitcast.87, bf16[256,3072]{1,0:T(8,128)(2,1)S(1)} %reshape.128, bf16[]{:T(256)} %constant.57.clone.1), kind=kCustom, calls=%fused_computation.19 | custom fusion | bytes 3145730 | tf_op jit(solution)/shard_map/scatter | solution.py:289
  164.6 4.1 %all-to-all-start.4 = ((bf16[8,64,3072]{2,1,0:T(8,128)(2,1)}), bf16[8,64,3072]{2,1,0:T(8,128)(2,1)S(1)}, u32[]{:S(2)}, u32[]{:S(2)}) async-start(bf16[8,64,3072]{2,1,0:T(8,128)(2,1)} %bitcast.28), calls=%async_computation.4 | async-start | bytes 6291456 | tf_op jit(solution)/shard_map/all_to_all | solution.py:291
  168.7 71.2 %all-to-all-done.4 = bf16[8,64,3072]{2,1,0:T(8,128)(2,1)S(1)} async-done(((bf16[8,64,3072]{2,1,0:T(8,128)(2,1)}), bf16[8,64,3072]{2,1,0:T(8,128)(2,1)S(1)}, u32[]{:S(2)}, u32[]{:S(2)}) %all-to-all-start.4) | async-done | bytes 3145760 | tf_op jit(solution)/shard_map/all_to_all | solution.py:291
  240.0 18.4 %fusion.4 = bf16[512,3072]{1,0:T(8,128)(2,1)} fusion(bf16[1,1536,3072]{2,1,0:T(8,128)(2,1)} %all-gather.5.cloned.1.call-done, bf16[512,3072]{1,0:T(8,128)(2,1)S(1)} %bitcast.64, bf16[1,1536,3072]{2,1,0:T(8,128)(2,1)} %all-gather.3.cloned.1.call-done), kind=kOutput, calls=%fused_computation.7 | convolution fusion | flops 9672327168 | bytes 25165824 | tf_op jit(solution)/shard_map/dot_general | solution.py:23
  258.4 4.0 %all-to-all-start.5 = ((bf16[8,64,3072]{2,1,0:T(8,128)(2,1)}), bf16[8,64,3072]{2,1,0:T(8,128)(2,1)S(1)}, u32[]{:S(2)}, u32[]{:S(2)}) async-start(bf16[8,64,3072]{2,1,0:T(8,128)(2,1)} %bitcast.65), calls=%async_computation.5 | async-start | bytes 6291456 | tf_op jit(solution)/shard_map/all_to_all | solution.py:299
  263.4 69.8 %all-to-all-done.5 = bf16[8,64,3072]{2,1,0:T(8,128)(2,1)S(1)} async-done(((bf16[8,64,3072]{2,1,0:T(8,128)(2,1)}), bf16[8,64,3072]{2,1,0:T(8,128)(2,1)S(1)}, u32[]{:S(2)}, u32[]{:S(2)}) %all-to-all-start.5) | async-done | bytes 3145760 | tf_op jit(solution)/shard_map/all_to_all | solution.py:299
  333.2 2.7 gather_fusion
  335.9 3.5 reshape.115
  339.5 4.5 %multiply_reduce_fusion = f32[128,3072]{1,0:T(8,128)S(1)} fusion(f32[128,2,3072]{2,1,0:T(2,128)S(1)} %reshape.115, f32[128,2]{1,0:T(8,128)S(1)} %copy.58), kind=kLoop, calls=%fused_computation.15 | loop fusion | flops 1179648 | bytes 4719616 | tf_op jit(solution)/shard_map/reduce_sum | solution.py:303
  (102 shorter events, 18.5 us)
Async XLA Ops:
  6.5 162.2 %all-gather.3.cloned.1.call-start = ((), (), s32[]{:S(2)}) async-start(), calls=%async_computation.6 | async-start | bytes 14155776 | tf_op jit(solution)/shard_map/all_gather | solution.py:295
  10.5 2.0 collective-permute-start
  14.7 26.6 %all-to-all-start.2 = ((bf16[4,3,256,128]{3,2,1,0:T(8,128)(2,1)}), bf16[4,3,256,128]{3,2,1,0:T(8,128)(2,1)S(1)}, u32[]{:S(2)}, u32[]{:S(2)}) async-start(bf16[4,3,256,128]{3,2,1,0:T(8,128)(2,1)} %maximum_select_fusion), calls=%async_computation.2 | async-start | bytes 1572864 | tf_op jit(solution)/shard_map/all_to_all | solution.py:151
  20.9 125.5 %collective-permute-start.2 = (bf16[768,3072]{1,0:T(8,128)(2,1)}, bf16[768,3072]{1,0:T(8,128)(2,1)}, u32[]{:S(2)}, u32[]{:S(2)}) collective-permute-start(bf16[768,3072]{1,0:T(8,128)(2,1)} %refs_0_.1), channel_id=1, source_target_pairs={{0,1},{1,0},{2,3},{3,2},{4,5},{5,4},{6,7},{7,6},{8,9},{9,8},{10,11... | collective-permute-start | bytes 14155784 | tf_op jit(solution)/shard_map/ppermute | solution.py:157
  41.3 28.1 %copy-start = (bf16[4,3,256,128]{3,2,1,0:T(8,128)(2,1)}, bf16[4,3,256,128]{3,2,1,0:T(8,128)(2,1)S(1)}, u32[]{:S(2)}) copy-start(bf16[4,3,256,128]{3,2,1,0:T(8,128)(2,1)S(1)} %all-to-all-done.2.query_ref.refs_0_.refs_1_) | copy-start | bytes 2359300
  41.3 67.2 %all-to-all-start = ((bf16[4,3,512,128]{3,2,1,0:T(8,128)(2,1)}), bf16[4,3,512,128]{3,2,1,0:T(8,128)(2,1)S(1)}, u32[]{:S(2)}, u32[]{:S(2)}) async-start(bf16[4,3,512,128]{3,2,1,0:T(8,128)(2,1)} %pad_maximum_fusion), calls=%async_computation | async-start | bytes 3145728 | tf_op jit(solution)/shard_map/all_to_all | solution.py:143
  44.9 123.8 %all-gather.5.cloned.1.call-start = ((), (), s32[]{:S(2)}) async-start(), calls=%async_computation.7 | async-start | bytes 14155776 | tf_op jit(solution)/shard_map/all_gather | solution.py:296
  47.4 67.0 %copy-start.13 = (s32[128,2]{0,1:T(2,128)S(1)}, s32[128,2]{0,1:T(2,128)}, u32[]{:S(2)}) copy-start(s32[128,2]{0,1:T(2,128)} %param.18) | copy-start | bytes 3076
  47.5 20.5 %collective-permute-start.3 = (bf16[128,3072]{1,0:T(8,128)(2,1)S(1)}, bf16[128,3072]{1,0:T(8,128)(2,1)S(1)}, u32[]{:S(2)}, u32[]{:S(2)}) collective-permute-start(bf16[128,3072]{1,0:T(8,128)(2,1)S(1)} %get-tuple-element.11), channel_id=1, source_target_pairs={{0,2},{2,0},{1,3},{3,1},{4,6},{6,4},{5,7},{7,5},{8,10},{10,8},{9,1... | collective-permute-start | bytes 2359304 | tf_op jit(solution)/shard_map/ppermute | solution.py:160
  49.0 35.9 %collective-permute-start.4 = (bf16[128,3072]{1,0:T(8,128)(2,1)S(1)}, bf16[128,3072]{1,0:T(8,128)(2,1)}, u32[]{:S(2)}, u32[]{:S(2)}) collective-permute-start(bf16[128,3072]{1,0:T(8,128)(2,1)S(1)} %get-tuple-element.10), channel_id=1, source_target_pairs={{0,2},{2,0},{1,3},{3,1},{4,6},{6,4},{5,7},{7,5},{8,10},{10,8},{9,1... | collective-permute-start | bytes 2359304 | tf_op jit(solution)/shard_map/ppermute | solution.py:160
  49.6 50.3 %collective-permute-start.5 = (bf16[128,3072]{1,0:T(8,128)(2,1)S(1)}, bf16[128,3072]{1,0:T(8,128)(2,1)}, u32[]{:S(2)}, u32[]{:S(2)}) collective-permute-start(bf16[128,3072]{1,0:T(8,128)(2,1)S(1)} %get-tuple-element.9), channel_id=1, source_target_pairs={{0,2},{2,0},{1,3},{3,1},{4,6},{6,4},{5,7},{7,5},{8,10},{10,8},{9,1... | collective-permute-start | bytes 2359304 | tf_op jit(solution)/shard_map/ppermute | solution.py:160
  67.9 33.6 %copy-start.5 = (bf16[128,3072]{1,0:T(8,128)(2,1)}, bf16[128,3072]{1,0:T(8,128)(2,1)S(1)}, u32[]{:S(2)}) copy-start(bf16[128,3072]{1,0:T(8,128)(2,1)S(1)} %collective-permute-done.3.refs_2_) | copy-start | bytes 2359300
  67.9 32.0 %collective-permute-start.6 = (bf16[128,3072]{1,0:T(8,128)(2,1)S(1)}, bf16[128,3072]{1,0:T(8,128)(2,1)S(1)}, u32[]{:S(2)}, u32[]{:S(2)}) collective-permute-start(bf16[128,3072]{1,0:T(8,128)(2,1)S(1)} %collective-permute-done.3.refs_2_), channel_id=1, source_target_pairs={{0,16},{16,0},{1,17},{17,1},{2,18},{18,2},{3,19},{19,3},{4,20},{20... | collective-permute-start | bytes 2359304 | tf_op jit(solution)/shard_map/ppermute | solution.py:162
  69.5 32.0 %collective-permute-start.1 = (bf16[4,3,256,128]{3,2,1,0:T(8,128)(2,1)S(1)}, bf16[4,3,256,128]{3,2,1,0:T(8,128)(2,1)S(1)}, u32[]{:S(2)}, u32[]{:S(2)}) collective-permute-start(bf16[4,3,256,128]{3,2,1,0:T(8,128)(2,1)S(1)} %all-to-all-done.2.query_ref.refs_0_.refs_1_), channel_id=1, source_target_pairs={{0,1},{1,0},{2,3},{3,2},{4,5},{5,4},{6,7},{7,6},{8,9},{9,8},{10,11... | collective-permute-start | bytes 2359304 | tf_op jit(solution)/shard_map/ppermute | solution.py:152
  84.9 47.3 %collective-permute-start.7 = (bf16[128,3072]{1,0:T(8,128)(2,1)}, bf16[128,3072]{1,0:T(8,128)(2,1)}, u32[]{:S(2)}, u32[]{:S(2)}) collective-permute-start(bf16[128,3072]{1,0:T(8,128)(2,1)} %collective-permute-done.4.refs_3_), channel_id=1, source_target_pairs={{0,16},{16,0},{1,17},{17,1},{2,18},{18,2},{3,19},{19,3},{4,20},{20... | collective-permute-start | bytes 2359304 | tf_op jit(solution)/shard_map/ppermute | solution.py:162
  99.9 32.9 %collective-permute-start.10 = (bf16[128,3072]{1,0:T(8,128)(2,1)}, bf16[128,3072]{1,0:T(8,128)(2,1)}, u32[]{:S(2)}, u32[]{:S(2)}) collective-permute-start(bf16[128,3072]{1,0:T(8,128)(2,1)} %collective-permute-done.4.refs_3_), channel_id=1, source_target_pairs={{0,1},{1,0},{2,3},{3,2},{4,5},{5,4},{6,7},{7,6},{8,9},{9,8},{10,11... | collective-permute-start | bytes 2359304 | tf_op jit(solution)/shard_map/ppermute | solution.py:164
  99.9 32.8 %collective-permute-start.8 = (bf16[128,3072]{1,0:T(8,128)(2,1)}, bf16[128,3072]{1,0:T(8,128)(2,1)}, u32[]{:S(2)}, u32[]{:S(2)}) collective-permute-start(bf16[128,3072]{1,0:T(8,128)(2,1)} %collective-permute-done.5.refs_4_), channel_id=1, source_target_pairs={{0,16},{16,0},{1,17},{17,1},{2,18},{18,2},{3,19},{19,3},{4,20},{20... | collective-permute-start | bytes 2359304 | tf_op jit(solution)/shard_map/ppermute | solution.py:162
  101.5 31.7 %collective-permute-start.11 = (bf16[128,3072]{1,0:T(8,128)(2,1)}, bf16[128,3072]{1,0:T(8,128)(2,1)}, u32[]{:S(2)}, u32[]{:S(2)}) collective-permute-start(bf16[128,3072]{1,0:T(8,128)(2,1)} %collective-permute-done.5.refs_4_), channel_id=1, source_target_pairs={{0,1},{1,0},{2,3},{3,2},{4,5},{5,4},{6,7},{7,6},{8,9},{9,8},{10,11... | collective-permute-start | bytes 2359304 | tf_op jit(solution)/shard_map/ppermute | solution.py:164
  108.6 6.8 %copy-start.3 = (bf16[4,3,512,128]{3,2,1,0:T(8,128)(2,1)}, bf16[4,3,512,128]{3,2,1,0:T(8,128)(2,1)S(1)}, u32[]{:S(2)}) copy-start(bf16[4,3,512,128]{3,2,1,0:T(8,128)(2,1)S(1)} %all-to-all-done.query_ref.refs_0_.refs_1_) | copy-start | bytes 4718596
  108.6 17.6 %all-to-all-start.3 = ((bf16[16,64,128]{2,1,0:T(8,128)(2,1)}), bf16[16,64,128]{2,1,0:T(8,128)(2,1)S(1)}, u32[]{:S(2)}, u32[]{:S(2)}) async-start(bf16[16,64,128]{2,1,0:T(8,128)(2,1)} %bitcast.77), calls=%async_computation.3 | async-start | bytes 524288 | tf_op jit(solution)/shard_map/all_to_all | solution.py:176
  115.4 16.8 %copy-start.6 = (bf16[128,3072]{1,0:T(8,128)(2,1)S(1)}, bf16[128,3072]{1,0:T(8,128)(2,1)}, u32[]{:S(2)}) copy-start(bf16[128,3072]{1,0:T(8,128)(2,1)} %copy-done.5) | copy-start | bytes 2359300
  126.2 20.3 %copy-start.4 = (bf16[16,64,128]{2,1,0:T(8,128)(2,1)}, bf16[16,64,128]{2,1,0:T(8,128)(2,1)S(1)}, u32[]{:S(2)}) copy-start(bf16[16,64,128]{2,1,0:T(8,128)(2,1)S(1)} %all-to-all-done.3) | copy-start | bytes 786436
  126.2 20.3 %all-to-all-start.1 = ((bf16[16,128,128]{2,1,0:T(8,128)(2,1)}), bf16[16,128,128]{2,1,0:T(8,128)(2,1)S(1)}, u32[]{:S(2)}, u32[]{:S(2)}) async-start(bf16[16,128,128]{2,1,0:T(8,128)(2,1)} %bitcast.84), calls=%async_computation.1 | async-start | bytes 1048576 | tf_op jit(solution)/shard_map/all_to_all | solution.py:168
  132.2 2.4 collective-permute-start.9
  132.7 3.1 collective-permute-start.12
  132.8 4.2 %collective-permute-start.13 = (bf16[128,3072]{1,0:T(8,128)(2,1)}, bf16[128,3072]{1,0:T(8,128)(2,1)}, u32[]{:S(2)}, u32[]{:S(2)}) collective-permute-start(bf16[128,3072]{1,0:T(8,128)(2,1)} %collective-permute-done.7.refs_6_), channel_id=1, source_target_pairs={{0,1},{1,0},{2,3},{3,2},{4,5},{5,4},{6,7},{7,6},{8,9},{9,8},{10,11... | collective-permute-start | bytes 2359304 | tf_op jit(solution)/shard_map/ppermute | solution.py:164
  133.2 4.9 %collective-permute-start.14 = (bf16[128,3072]{1,0:T(8,128)(2,1)}, bf16[128,3072]{1,0:T(8,128)(2,1)}, u32[]{:S(2)}, u32[]{:S(2)}) collective-permute-start(bf16[128,3072]{1,0:T(8,128)(2,1)} %collective-permute-done.8.refs_7_), channel_id=1, source_target_pairs={{0,1},{1,0},{2,3},{3,2},{4,5},{5,4},{6,7},{7,6},{8,9},{9,8},{10,11... | collective-permute-start | bytes 2359304 | tf_op jit(solution)/shard_map/ppermute | solution.py:164
  134.7 11.8 %copy-start.8 = (bf16[128,3072]{1,0:T(8,128)(2,1)}, bf16[128,3072]{1,0:T(8,128)(2,1)S(1)}, u32[]{:S(2)}) copy-start(bf16[128,3072]{1,0:T(8,128)(2,1)S(1)} %collective-permute-done.9.refs_8_) | copy-start | bytes 2359300
  135.8 10.7 %copy-start.9 = (bf16[128,3072]{1,0:T(8,128)(2,1)}, bf16[128,3072]{1,0:T(8,128)(2,1)S(1)}, u32[]{:S(2)}) copy-start(bf16[128,3072]{1,0:T(8,128)(2,1)S(1)} %collective-permute-done.12.refs_11_) | copy-start | bytes 2359300
  164.6 75.3 %all-to-all-start.4 = ((bf16[8,64,3072]{2,1,0:T(8,128)(2,1)}), bf16[8,64,3072]{2,1,0:T(8,128)(2,1)S(1)}, u32[]{:S(2)}, u32[]{:S(2)}) async-start(bf16[8,64,3072]{2,1,0:T(8,128)(2,1)} %bitcast.28), calls=%async_computation.4 | async-start | bytes 6291456 | tf_op jit(solution)/shard_map/all_to_all | solution.py:291
  258.4 4.9 %copy-start.14 = (f32[128,2]{0,1:T(2,128)S(1)}, f32[128,2]{0,1:T(2,128)}, u32[]{:S(2)}) copy-start(f32[128,2]{0,1:T(2,128)} %param.19) | copy-start | bytes 3076
  258.4 74.8 %all-to-all-start.5 = ((bf16[8,64,3072]{2,1,0:T(8,128)(2,1)}), bf16[8,64,3072]{2,1,0:T(8,128)(2,1)S(1)}, u32[]{:S(2)}, u32[]{:S(2)}) async-start(bf16[8,64,3072]{2,1,0:T(8,128)(2,1)} %bitcast.65), calls=%async_computation.5 | async-start | bytes 6291456 | tf_op jit(solution)/shard_map/all_to_all | solution.py:299
  (6 other events, 10.6 us)
Sparse Core Ops, SparseCore 0:
  8.9 27.0 all-gather.2
  47.3 23.0 all-gather.4

commit v2 on v1

--- a/solution.py
+++ b/solution.py
@@ -7,6 +7,7 @@
 from jax.experimental import pallas as pl
 from jax.experimental.pallas import tpu as pltpu
 from jax.sharding import PartitionSpec as P
+
 
 HEAD_DIM = 128
 TOP = 2
@@ -77,6 +78,23 @@
     )(*operands)
 
 
+def pack_kernel(planes, half, core_ref, q_ref, k_ref, v_ref, first_ref, kept_ref, sent_ref):
+    core = core_ref[0]
+    for which, ref in enumerate((q_ref, k_ref, v_ref)):
+        heads = ref.shape[1] // HEAD_DIM
+        for h in range(heads):
+            columns = slice(h * HEAD_DIM, (h + 1) * HEAD_DIM)
+            if h < planes:
+                first_ref[h, which] = ref[:, columns]
+                continue
+            for out, side in ((kept_ref, core), (sent_ref, 1 - core)):
+                for j in range(ref.shape[0] // (2 * half)):
+                    start = pl.multiple_of(j * 2 * half + side * half, half)
+                    out[h - planes, which, j * half : (j + 1) * half] = ref[
+                        pl.ds(start, half), columns
+                    ]
+
+
 def swap(axis):
     return partial(lax.ppermute, axis_name=axis, perm=[(0, 1), (1, 0)])
 
@@ -130,20 +148,22 @@
     blocks = lax.axis_size(("expert", "fsdp"))
     token_rows = tokens.shape[0]
     half = token_rows // 2
-    mine = [t.reshape(query_rows, heads, HEAD_DIM) for t in (queries, keys, values)]
-
-    first = jnp.stack([t[:, :planes].transpose(1, 0, 2) for t in mine], axis=1)
-    other = jnp.stack(
-        [
-            t[:, planes:].reshape(blocks, 2, half, heads - planes, HEAD_DIM).transpose(1, 3, 0, 2, 4)
-            for t in mine
+    core = lax.axis_index("fsdp")
+    vmem = pl.BlockSpec(memory_space=pltpu.VMEM)
+    own = (heads - planes, 3, blocks * half, HEAD_DIM)
+    first, kept, sent = pl.pallas_call(
+        partial(pack_kernel, planes, half),
+        in_specs=[pl.BlockSpec(memory_space=pltpu.SMEM)] + [vmem] * 3,
+        out_specs=[vmem] * 3,
+        out_shape=[
+            jax.ShapeDtypeStruct((planes, 3, query_rows, HEAD_DIM), jnp.bfloat16),
+            jax.ShapeDtypeStruct(own, jnp.bfloat16),
+            jax.ShapeDtypeStruct(own, jnp.bfloat16),
         ],
-        axis=2,
-    ).reshape(2, heads - planes, 3, blocks * half, HEAD_DIM)
+        compiler_params=pltpu.CompilerParams(vmem_limit_bytes=VMEM_LIMIT),
+        name="pack",
+    )(core.reshape(1), queries, keys, values)
     first_in = lax.all_to_all(first, "seq", split_axis=0, concat_axis=0, tiled=True)
-    core = lax.axis_index("fsdp")
-    sent = lax.dynamic_index_in_dim(other, 1 - core, 0, keepdims=False)
-    kept = lax.dynamic_index_in_dim(other, core, 0, keepdims=False)
     came = swap("fsdp")(sent)
     second = jnp.where(
         core == 0, jnp.concatenate([kept, came], 0), jnp.concatenate([came, kept], 0)
@@ -183,14 +203,6 @@
 
     col = lax.axis_index("expert")
     full_heads = planes * blocks
-
-    def slots(x, c, which):
-        return [
-            p * blocks + 2 * x + c
-            if p < planes
-            else full_heads + (2 * c + p - planes) * 2 + x
-            for p in which
-        ]
 
     everything = jnp.arange(heads)
 
@@ -214,7 +226,6 @@
     counts = tuple(p.shape[0] // HEAD_DIM for p in pieces)
     width = out_weight.shape[1]
     total = sum(counts)
-    vmem = pl.BlockSpec(memory_space=pltpu.VMEM)
     return pl.pallas_call(
         partial(project_kernel, counts),
         in_specs=[pl.BlockSpec(memory_space=pltpu.SMEM)]
@@ -334,6 +345,7 @@
         P(("group", "seq", "expert", "fsdp"), None),
         P(("group", "seq", "expert", "fsdp"), None),
     )
+
     return jax.shard_map(
         per_device,
         mesh=mesh,

time: 353 us -> 353 us (level)
  local copies, waits for them, and re-layouts: 25.5 us -> 19.4 us
  waiting for transfers between devices: 218 us -> 222 us
    unnamed x38 -> x28, local copies, waits for them, and re-layouts: 6.08 us -> 1.73 us
    all_to_all x1, waiting for transfers between devices: 16.1 us -> 20.4 us  [moved_heads_attention(): lax.all_to_all(second, 'seq', split_axis=0, concat_axis=0, tiled=True)]
  transfers between devices with their start and end apart: 23 -> 23, of which waited for: 11 -> 11; matrix products, arithmetic and copies ran while one was open for 6% -> 4% of each run, Pallas kernels for 8% -> 9%
where the time goes in v2:
time: 353 us; the launch traced here: 352 us
  waiting for transfers between devices  222 us (63%)
  starting transfers between devices  39.8 us (11%)
  Pallas kernels  30.2 us (9%)
  local copies, waits for them, and re-layouts  19.4 us (5%)
  matrix products  18.5 us (5%)
  between operations  13.7 us (4%)
  other arithmetic  8.44 us (2%)
    all_to_all x1, waiting for transfers between devices, sent_tokens_experts(): lax.all_to_all(outgoing, ('seq', 'expert'), split_axis=0, concat_axis=0,...  71.2 us
    all_to_all x1, waiting for transfers between devices, sent_tokens_experts(): lax.all_to_all(results, ('seq', 'expert'), split_axis=0, concat_axis=0, t...  69.8 us
    ppermute x3, waiting for transfers between devices, moved_heads_attention(): from_x.append(swap('expert')(to_x[i * HEAD_DIM:(i + 1) * HEAD_DIM]))  45.8 us
    all_to_all x1, waiting for transfers between devices, moved_heads_attention(): lax.all_to_all(second, 'seq', split_axis=0, concat_axis=0, tiled=True)  20.4 us
    dot_general x1, matrix products, expert_block(): jnp.dot(hidden_act.astype(jnp.bfloat16), weight_out, preferred_element_ty...  18.5 us
    pallas_call x2, Pallas kernels, attention(): pl.pallas_call(partial(attention_kernel, len(packs)), grid=(planes * per,...  17 us
    pallas_call x1, Pallas kernels, moved_heads_attention(): pl.pallas_call(partial(project_kernel, counts), in_specs=[pl.BlockSpec(me...  9.82 us
    all_to_all x1, waiting for transfers between devices, moved_heads_attention(): lax.all_to_all(first_out.reshape(planes * blocks, token_rows, HEAD_DIM),...  8.32 us
  transfers between devices with their start and end apart: 23, of which 11 were waited for; matrix products, arithmetic and copies ran while one was open for 4% of the time, Pallas kernels for 9%

profile of v2, /device:TPU:0, one launch (start us, length us, event | category | flops | bytes accessed | tf_op | source)
XLA Modules:
  0.0 352.1 jit_solution(4692818971104412578)
XLA Ops:
  7.3 3.4 pack.1
  11.2 1.6 collective-permute-done
  12.7 2.1 maximum_select_fusion
  14.8 6.2 %all-to-all-start.2 = ((bf16[4,3,256,128]{3,2,1,0:T(8,128)(2,1)}), bf16[4,3,256,128]{3,2,1,0:T(8,128)(2,1)S(1)}, u32[]{:S(2)}, u32[]{:S(2)}) async-start(bf16[4,3,256,128]{3,2,1,0:T(8,128)(2,1)} %maximum_select_fusion), calls=%async_computation.2 | async-start | bytes 1572864 | tf_op jit(solution)/shard_map/all_to_all | solution.py:171
  21.1 20.4 %all-to-all-done.2.query_ref.refs_0_.refs_1_ = bf16[4,3,256,128]{3,2,1,0:T(8,128)(2,1)S(1)} async-done(((bf16[4,3,256,128]{3,2,1,0:T(8,128)(2,1)}), bf16[4,3,256,128]{3,2,1,0:T(8,128)(2,1)S(1)}, u32[]{:S(2)}, u32[]{:S(2)}) %all-to-all-start.2) | async-done | bytes 786464 | tf_op jit(solution)/shard_map/all_to_all | solution.py:171
  41.5 3.6 %all-to-all-start = ((bf16[4,3,512,128]{3,2,1,0:T(8,128)(2,1)}), bf16[4,3,512,128]{3,2,1,0:T(8,128)(2,1)S(1)}, u32[]{:S(2)}, u32[]{:S(2)}) async-start(bf16[4,3,512,128]{3,2,1,0:T(8,128)(2,1)} %get-tuple-element.10), calls=%async_computation | async-start | bytes 3145728 | tf_op jit(solution)/shard_map/all_to_all | solution.py:166
  45.8 1.8 constant_dynamic-slice_fusion.2
  47.6 1.6 collective-permute-start.3
  49.7 1.5 collective-permute-start.5
  51.2 16.9 %collective-permute-done.3.refs_2_ = bf16[128,3072]{1,0:T(8,128)(2,1)S(1)} collective-permute-done((bf16[128,3072]{1,0:T(8,128)(2,1)S(1)}, bf16[128,3072]{1,0:T(8,128)(2,1)S(1)}, u32[]{:S(2)}, u32[]{:S(2)}) %collective-permute-start.3) | collective-permute-done | bytes 786464 | tf_op jit(solution)/shard_map/ppermute | solution.py:180
  68.1 1.5 collective-permute-start.6
  69.6 15.4 %collective-permute-done.4.refs_3_ = bf16[128,3072]{1,0:T(8,128)(2,1)} collective-permute-done((bf16[128,3072]{1,0:T(8,128)(2,1)S(1)}, bf16[128,3072]{1,0:T(8,128)(2,1)}, u32[]{:S(2)}, u32[]{:S(2)}) %collective-permute-start.4) | collective-permute-done | bytes 786464 | tf_op jit(solution)/shard_map/ppermute | solution.py:180
  85.0 1.5 collective-permute-start.7
  86.6 13.5 %collective-permute-done.5.refs_4_ = bf16[128,3072]{1,0:T(8,128)(2,1)} collective-permute-done((bf16[128,3072]{1,0:T(8,128)(2,1)S(1)}, bf16[128,3072]{1,0:T(8,128)(2,1)}, u32[]{:S(2)}, u32[]{:S(2)}) %collective-permute-start.5) | collective-permute-done | bytes 786464 | tf_op jit(solution)/shard_map/ppermute | solution.py:180
  100.0 1.6 collective-permute-start.8
  102.5 6.2 %attention.3 = bf16[1024,128]{1,0:T(8,128)(2,1)} custom-call(bf16[4,3,256,128]{3,2,1,0:T(8,128)(2,1)} %copy-done, bf16[4,3,256,128]{3,2,1,0:T(8,128)(2,1)} %copy-done, bf16[4,3,256,128]{3,2,1,0:T(8,128)(2,1)} %copy-done, bf16[4,3,256,128]{3,2,1,0:T(8,128)(2,1)} %copy-done.1, bf16[4,3,256,128]{3,2,1,0:T(8,128)(2,1)} %copy-done.1), custom_call_target="tpu_custom_call" | custom-call | flops 1073741824 | bytes 1572864 | tf_op jit(solution)/shard_map/attention/pallas_call | solution.py:65
  108.7 5.8 %all-to-all-start.3 = ((bf16[16,64,128]{2,1,0:T(8,128)(2,1)}), bf16[16,64,128]{2,1,0:T(8,128)(2,1)S(1)}, u32[]{:S(2)}, u32[]{:S(2)}) async-start(bf16[16,64,128]{2,1,0:T(8,128)(2,1)} %bitcast.38), calls=%async_computation.3 | async-start | bytes 524288 | tf_op jit(solution)/shard_map/all_to_all | solution.py:196
  115.6 10.8 %attention.2 = bf16[2048,128]{1,0:T(8,128)(2,1)} custom-call(bf16[4,3,512,128]{3,2,1,0:T(8,128)(2,1)} %copy-done.3, bf16[4,3,512,128]{3,2,1,0:T(8,128)(2,1)} %copy-done.3, bf16[4,3,512,128]{3,2,1,0:T(8,128)(2,1)} %copy-done.3), custom_call_target="tpu_custom_call" | custom-call | flops 2147483648 | bytes 2097152 | tf_op jit(solution)/shard_map/attention/pallas_call | solution.py:65
  126.4 6.0 %all-to-all-start.1 = ((bf16[16,128,128]{2,1,0:T(8,128)(2,1)}), bf16[16,128,128]{2,1,0:T(8,128)(2,1)S(1)}, u32[]{:S(2)}, u32[]{:S(2)}) async-start(bf16[16,128,128]{2,1,0:T(8,128)(2,1)} %bitcast.39), calls=%async_computation.1 | async-start | bytes 1048576 | tf_op jit(solution)/shard_map/all_to_all | solution.py:188
  134.8 1.3 collective-permute-done.12.refs_11_
  138.3 8.3 %all-to-all-done.1.full_ref = bf16[16,128,128]{2,1,0:T(8,128)(2,1)S(1)} async-done(((bf16[16,128,128]{2,1,0:T(8,128)(2,1)}), bf16[16,128,128]{2,1,0:T(8,128)(2,1)S(1)}, u32[]{:S(2)}, u32[]{:S(2)}) %all-to-all-start.1) | async-done | bytes 524320 | tf_op jit(solution)/shard_map/all_to_all | solution.py:188
  147.5 9.8 %project.1 = (bf16[128,3072]{1,0:T(8,128)(2,1)}, bf16[128,3072]{1,0:T(8,128)(2,1)}) custom-call(s32[24]{0:T(128)} %concatenate.9.slots_ref, bf16[16,128,128]{2,1,0:T(8,128)(2,1)} %copy-done.2, bf16[8,128,128]{2,1,0:T(8,128)(2,1)} %bitcast.37, bf16[128,3072]{1,0:T(8,128)(2,1)} %tokens_ref.1, f32[3,3072]{1,0:T(4,128)} %mod_ref.1, bf16[768,3072]{1,0:T(8,128)(2,1)} %refs_0_.1, ...), custom_call_target="tpu_custom_call" | custom-call | flops 2415919104 | bytes 18874368 | tf_op jit(solution)/shard_map/project/pallas_call | solution.py:229
  157.3 1.9 broadcast_in_dim.5
  159.9 4.9 %scatter_custom_fusion = bf16[512,3072]{1,0:T(8,128)(2,1)} fusion(s32[256]{0:T(256)S(1)} %bitcast.41, bf16[256,3072]{1,0:T(8,128)(2,1)S(1)} %reshape.101, bf16[]{:T(256)} %constant.50.clone.1), kind=kCustom, calls=%fused_computation.18 | custom fusion | bytes 3145730 | tf_op jit(solution)/shard_map/scatter | solution.py:300
  164.8 4.1 %all-to-all-start.4 = ((bf16[8,64,3072]{2,1,0:T(8,128)(2,1)}), bf16[8,64,3072]{2,1,0:T(8,128)(2,1)S(1)}, u32[]{:S(2)}, u32[]{:S(2)}) async-start(bf16[8,64,3072]{2,1,0:T(8,128)(2,1)} %bitcast.9), calls=%async_computation.4 | async-start | bytes 6291456 | tf_op jit(solution)/shard_map/all_to_all | solution.py:302
  168.9 71.2 %all-to-all-done.4 = bf16[8,64,3072]{2,1,0:T(8,128)(2,1)S(1)} async-done(((bf16[8,64,3072]{2,1,0:T(8,128)(2,1)}), bf16[8,64,3072]{2,1,0:T(8,128)(2,1)S(1)}, u32[]{:S(2)}, u32[]{:S(2)}) %all-to-all-start.4) | async-done | bytes 3145760 | tf_op jit(solution)/shard_map/all_to_all | solution.py:302
  240.2 18.5 %fusion.4 = bf16[512,3072]{1,0:T(8,128)(2,1)} fusion(bf16[1,1536,3072]{2,1,0:T(8,128)(2,1)} %all-gather.5.cloned.1.call-done, bf16[512,3072]{1,0:T(8,128)(2,1)S(1)} %bitcast.35, bf16[1,1536,3072]{2,1,0:T(8,128)(2,1)} %all-gather.3.cloned.1.call-done), kind=kOutput, calls=%fused_computation.7 | convolution fusion | flops 9672327168 | bytes 25165824 | tf_op jit(solution)/shard_map/dot_general | solution.py:24
  258.6 4.0 %all-to-all-start.5 = ((bf16[8,64,3072]{2,1,0:T(8,128)(2,1)}), bf16[8,64,3072]{2,1,0:T(8,128)(2,1)S(1)}, u32[]{:S(2)}, u32[]{:S(2)}) async-start(bf16[8,64,3072]{2,1,0:T(8,128)(2,1)} %bitcast.36), calls=%async_computation.5 | async-start | bytes 6291456 | tf_op jit(solution)/shard_map/all_to_all | solution.py:310
  263.6 69.8 %all-to-all-done.5 = bf16[8,64,3072]{2,1,0:T(8,128)(2,1)S(1)} async-done(((bf16[8,64,3072]{2,1,0:T(8,128)(2,1)}), bf16[8,64,3072]{2,1,0:T(8,128)(2,1)S(1)}, u32[]{:S(2)}, u32[]{:S(2)}) %all-to-all-start.5) | async-done | bytes 3145760 | tf_op jit(solution)/shard_map/all_to_all | solution.py:310
  333.4 2.7 gather_fusion
  336.1 3.5 reshape.88
  339.7 4.5 %multiply_reduce_fusion = f32[128,3072]{1,0:T(8,128)S(1)} fusion(f32[128,2,3072]{2,1,0:T(2,128)S(1)} %reshape.88, f32[128,2]{1,0:T(8,128)S(1)} %copy.15), kind=kLoop, calls=%fused_computation.15 | loop fusion | flops 1179648 | bytes 4719616 | tf_op jit(solution)/shard_map/reduce_sum | solution.py:314
  (76 shorter events, 12.5 us)
Async XLA Ops:
  6.5 162.4 %all-gather.3.cloned.1.call-start = ((), (), s32[]{:S(2)}) async-start(), calls=%async_computation.6 | async-start | bytes 14155776 | tf_op jit(solution)/shard_map/all_gather | solution.py:306
  10.7 2.1 collective-permute-start
  14.8 26.6 %all-to-all-start.2 = ((bf16[4,3,256,128]{3,2,1,0:T(8,128)(2,1)}), bf16[4,3,256,128]{3,2,1,0:T(8,128)(2,1)S(1)}, u32[]{:S(2)}, u32[]{:S(2)}) async-start(bf16[4,3,256,128]{3,2,1,0:T(8,128)(2,1)} %maximum_select_fusion), calls=%async_computation.2 | async-start | bytes 1572864 | tf_op jit(solution)/shard_map/all_to_all | solution.py:171
  21.1 125.6 %collective-permute-start.2 = (bf16[768,3072]{1,0:T(8,128)(2,1)}, bf16[768,3072]{1,0:T(8,128)(2,1)}, u32[]{:S(2)}, u32[]{:S(2)}) collective-permute-start(bf16[768,3072]{1,0:T(8,128)(2,1)} %refs_0_.1), channel_id=1, source_target_pairs={{0,1},{1,0},{2,3},{3,2},{4,5},{5,4},{6,7},{7,6},{8,9},{9,8},{10,11... | collective-permute-start | bytes 14155784 | tf_op jit(solution)/shard_map/ppermute | solution.py:177
  41.5 28.1 %copy-start = (bf16[4,3,256,128]{3,2,1,0:T(8,128)(2,1)}, bf16[4,3,256,128]{3,2,1,0:T(8,128)(2,1)S(1)}, u32[]{:S(2)}) copy-start(bf16[4,3,256,128]{3,2,1,0:T(8,128)(2,1)S(1)} %all-to-all-done.2.query_ref.refs_0_.refs_1_) | copy-start | bytes 2359300
  41.5 67.2 %all-to-all-start = ((bf16[4,3,512,128]{3,2,1,0:T(8,128)(2,1)}), bf16[4,3,512,128]{3,2,1,0:T(8,128)(2,1)S(1)}, u32[]{:S(2)}, u32[]{:S(2)}) async-start(bf16[4,3,512,128]{3,2,1,0:T(8,128)(2,1)} %get-tuple-element.10), calls=%async_computation | async-start | bytes 3145728 | tf_op jit(solution)/shard_map/all_to_all | solution.py:166
  45.1 123.9 %all-gather.5.cloned.1.call-start = ((), (), s32[]{:S(2)}) async-start(), calls=%async_computation.7 | async-start | bytes 14155776 | tf_op jit(solution)/shard_map/all_gather | solution.py:307
  47.6 67.0 %copy-start.11 = (s32[128,2]{0,1:T(2,128)S(1)}, s32[128,2]{0,1:T(2,128)}, u32[]{:S(2)}) copy-start(s32[128,2]{0,1:T(2,128)} %param.18) | copy-start | bytes 3076
  47.6 20.5 %collective-permute-start.3 = (bf16[128,3072]{1,0:T(8,128)(2,1)S(1)}, bf16[128,3072]{1,0:T(8,128)(2,1)S(1)}, u32[]{:S(2)}, u32[]{:S(2)}) collective-permute-start(bf16[128,3072]{1,0:T(8,128)(2,1)S(1)} %get-tuple-element.17), channel_id=1, source_target_pairs={{0,2},{2,0},{1,3},{3,1},{4,6},{6,4},{5,7},{7,5},{8,10},{10,8},{9,1... | collective-permute-start | bytes 2359304 | tf_op jit(solution)/shard_map/ppermute | solution.py:180
  49.2 35.9 %collective-permute-start.4 = (bf16[128,3072]{1,0:T(8,128)(2,1)S(1)}, bf16[128,3072]{1,0:T(8,128)(2,1)}, u32[]{:S(2)}, u32[]{:S(2)}) collective-permute-start(bf16[128,3072]{1,0:T(8,128)(2,1)S(1)} %get-tuple-element.16), channel_id=1, source_target_pairs={{0,2},{2,0},{1,3},{3,1},{4,6},{6,4},{5,7},{7,5},{8,10},{10,8},{9,1... | collective-permute-start | bytes 2359304 | tf_op jit(solution)/shard_map/ppermute | solution.py:180
  49.7 50.3 %collective-permute-start.5 = (bf16[128,3072]{1,0:T(8,128)(2,1)S(1)}, bf16[128,3072]{1,0:T(8,128)(2,1)}, u32[]{:S(2)}, u32[]{:S(2)}) collective-permute-start(bf16[128,3072]{1,0:T(8,128)(2,1)S(1)} %get-tuple-element.15), channel_id=1, source_target_pairs={{0,2},{2,0},{1,3},{3,1},{4,6},{6,4},{5,7},{7,5},{8,10},{10,8},{9,1... | collective-permute-start | bytes 2359304 | tf_op jit(solution)/shard_map/ppermute | solution.py:180
  68.1 33.6 %copy-start.5 = (bf16[128,3072]{1,0:T(8,128)(2,1)}, bf16[128,3072]{1,0:T(8,128)(2,1)S(1)}, u32[]{:S(2)}) copy-start(bf16[128,3072]{1,0:T(8,128)(2,1)S(1)} %collective-permute-done.3.refs_2_) | copy-start | bytes 2359300
  68.1 32.0 %collective-permute-start.6 = (bf16[128,3072]{1,0:T(8,128)(2,1)S(1)}, bf16[128,3072]{1,0:T(8,128)(2,1)S(1)}, u32[]{:S(2)}, u32[]{:S(2)}) collective-permute-start(bf16[128,3072]{1,0:T(8,128)(2,1)S(1)} %collective-permute-done.3.refs_2_), channel_id=1, source_target_pairs={{0,16},{16,0},{1,17},{17,1},{2,18},{18,2},{3,19},{19,3},{4,20},{20... | collective-permute-start | bytes 2359304 | tf_op jit(solution)/shard_map/ppermute | solution.py:182
  69.6 32.0 %collective-permute-start.1 = (bf16[4,3,256,128]{3,2,1,0:T(8,128)(2,1)S(1)}, bf16[4,3,256,128]{3,2,1,0:T(8,128)(2,1)S(1)}, u32[]{:S(2)}, u32[]{:S(2)}) collective-permute-start(bf16[4,3,256,128]{3,2,1,0:T(8,128)(2,1)S(1)} %all-to-all-done.2.query_ref.refs_0_.refs_1_), channel_id=1, source_target_pairs={{0,1},{1,0},{2,3},{3,2},{4,5},{5,4},{6,7},{7,6},{8,9},{9,8},{10,11... | collective-permute-start | bytes 2359304 | tf_op jit(solution)/shard_map/ppermute | solution.py:172
  85.0 47.4 %collective-permute-start.7 = (bf16[128,3072]{1,0:T(8,128)(2,1)}, bf16[128,3072]{1,0:T(8,128)(2,1)}, u32[]{:S(2)}, u32[]{:S(2)}) collective-permute-start(bf16[128,3072]{1,0:T(8,128)(2,1)} %collective-permute-done.4.refs_3_), channel_id=1, source_target_pairs={{0,16},{16,0},{1,17},{17,1},{2,18},{18,2},{3,19},{19,3},{4,20},{20... | collective-permute-start | bytes 2359304 | tf_op jit(solution)/shard_map/ppermute | solution.py:182
  100.0 33.0 %collective-permute-start.10 = (bf16[128,3072]{1,0:T(8,128)(2,1)}, bf16[128,3072]{1,0:T(8,128)(2,1)}, u32[]{:S(2)}, u32[]{:S(2)}) collective-permute-start(bf16[128,3072]{1,0:T(8,128)(2,1)} %collective-permute-done.4.refs_3_), channel_id=1, source_target_pairs={{0,1},{1,0},{2,3},{3,2},{4,5},{5,4},{6,7},{7,6},{8,9},{9,8},{10,11... | collective-permute-start | bytes 2359304 | tf_op jit(solution)/shard_map/ppermute | solution.py:184
  100.0 32.8 %collective-permute-start.8 = (bf16[128,3072]{1,0:T(8,128)(2,1)}, bf16[128,3072]{1,0:T(8,128)(2,1)}, u32[]{:S(2)}, u32[]{:S(2)}) collective-permute-start(bf16[128,3072]{1,0:T(8,128)(2,1)} %collective-permute-done.5.refs_4_), channel_id=1, source_target_pairs={{0,16},{16,0},{1,17},{17,1},{2,18},{18,2},{3,19},{19,3},{4,20},{20... | collective-permute-start | bytes 2359304 | tf_op jit(solution)/shard_map/ppermute | solution.py:182
  101.7 31.8 %collective-permute-start.11 = (bf16[128,3072]{1,0:T(8,128)(2,1)}, bf16[128,3072]{1,0:T(8,128)(2,1)}, u32[]{:S(2)}, u32[]{:S(2)}) collective-permute-start(bf16[128,3072]{1,0:T(8,128)(2,1)} %collective-permute-done.5.refs_4_), channel_id=1, source_target_pairs={{0,1},{1,0},{2,3},{3,2},{4,5},{5,4},{6,7},{7,6},{8,9},{9,8},{10,11... | collective-permute-start | bytes 2359304 | tf_op jit(solution)/shard_map/ppermute | solution.py:184
  108.7 6.8 %copy-start.3 = (bf16[4,3,512,128]{3,2,1,0:T(8,128)(2,1)}, bf16[4,3,512,128]{3,2,1,0:T(8,128)(2,1)S(1)}, u32[]{:S(2)}) copy-start(bf16[4,3,512,128]{3,2,1,0:T(8,128)(2,1)S(1)} %all-to-all-done.query_ref.refs_0_.refs_1_) | copy-start | bytes 4718596
  108.7 17.6 %all-to-all-start.3 = ((bf16[16,64,128]{2,1,0:T(8,128)(2,1)}), bf16[16,64,128]{2,1,0:T(8,128)(2,1)S(1)}, u32[]{:S(2)}, u32[]{:S(2)}) async-start(bf16[16,64,128]{2,1,0:T(8,128)(2,1)} %bitcast.38), calls=%async_computation.3 | async-start | bytes 524288 | tf_op jit(solution)/shard_map/all_to_all | solution.py:196
  115.6 16.8 %copy-start.6 = (bf16[128,3072]{1,0:T(8,128)(2,1)S(1)}, bf16[128,3072]{1,0:T(8,128)(2,1)}, u32[]{:S(2)}) copy-start(bf16[128,3072]{1,0:T(8,128)(2,1)} %copy-done.5) | copy-start | bytes 2359300
  115.6 17.3 %copy-start.8 = (bf16[128,3072]{1,0:T(8,128)(2,1)S(1)}, bf16[128,3072]{1,0:T(8,128)(2,1)}, u32[]{:S(2)}) copy-start(bf16[128,3072]{1,0:T(8,128)(2,1)} %copy-done.7) | copy-start | bytes 2359300
  126.4 20.3 %copy-start.4 = (bf16[16,64,128]{2,1,0:T(8,128)(2,1)}, bf16[16,64,128]{2,1,0:T(8,128)(2,1)S(1)}, u32[]{:S(2)}) copy-start(bf16[16,64,128]{2,1,0:T(8,128)(2,1)S(1)} %all-to-all-done.3) | copy-start | bytes 786436
  126.4 20.3 %all-to-all-start.1 = ((bf16[16,128,128]{2,1,0:T(8,128)(2,1)}), bf16[16,128,128]{2,1,0:T(8,128)(2,1)S(1)}, u32[]{:S(2)}, u32[]{:S(2)}) async-start(bf16[16,128,128]{2,1,0:T(8,128)(2,1)} %bitcast.39), calls=%async_computation.1 | async-start | bytes 1048576 | tf_op jit(solution)/shard_map/all_to_all | solution.py:188
  132.4 2.4 collective-permute-start.9
  132.9 3.2 collective-permute-start.12
  133.0 4.2 %collective-permute-start.13 = (bf16[128,3072]{1,0:T(8,128)(2,1)}, bf16[128,3072]{1,0:T(8,128)(2,1)}, u32[]{:S(2)}, u32[]{:S(2)}) collective-permute-start(bf16[128,3072]{1,0:T(8,128)(2,1)} %collective-permute-done.7.refs_6_), channel_id=1, source_target_pairs={{0,1},{1,0},{2,3},{3,2},{4,5},{5,4},{6,7},{7,6},{8,9},{9,8},{10,11... | collective-permute-start | bytes 2359304 | tf_op jit(solution)/shard_map/ppermute | solution.py:184
  133.4 4.9 %collective-permute-start.14 = (bf16[128,3072]{1,0:T(8,128)(2,1)}, bf16[128,3072]{1,0:T(8,128)(2,1)}, u32[]{:S(2)}, u32[]{:S(2)}) collective-permute-start(bf16[128,3072]{1,0:T(8,128)(2,1)} %collective-permute-done.8.refs_7_), channel_id=1, source_target_pairs={{0,1},{1,0},{2,3},{3,2},{4,5},{5,4},{6,7},{7,6},{8,9},{9,8},{10,11... | collective-permute-start | bytes 2359304 | tf_op jit(solution)/shard_map/ppermute | solution.py:184
  134.8 11.8 %copy-start.9 = (bf16[128,3072]{1,0:T(8,128)(2,1)}, bf16[128,3072]{1,0:T(8,128)(2,1)S(1)}, u32[]{:S(2)}) copy-start(bf16[128,3072]{1,0:T(8,128)(2,1)S(1)} %collective-permute-done.9.refs_8_) | copy-start | bytes 2359300
  164.8 75.3 %all-to-all-start.4 = ((bf16[8,64,3072]{2,1,0:T(8,128)(2,1)}), bf16[8,64,3072]{2,1,0:T(8,128)(2,1)S(1)}, u32[]{:S(2)}, u32[]{:S(2)}) async-start(bf16[8,64,3072]{2,1,0:T(8,128)(2,1)} %bitcast.9), calls=%async_computation.4 | async-start | bytes 6291456 | tf_op jit(solution)/shard_map/all_to_all | solution.py:302
  258.6 4.9 %copy-start.12 = (f32[128,2]{0,1:T(2,128)S(1)}, f32[128,2]{0,1:T(2,128)}, u32[]{:S(2)}) copy-start(f32[128,2]{0,1:T(2,128)} %param.19) | copy-start | bytes 3076
  258.6 74.8 %all-to-all-start.5 = ((bf16[8,64,3072]{2,1,0:T(8,128)(2,1)}), bf16[8,64,3072]{2,1,0:T(8,128)(2,1)S(1)}, u32[]{:S(2)}, u32[]{:S(2)}) async-start(bf16[8,64,3072]{2,1,0:T(8,128)(2,1)} %bitcast.36), calls=%async_computation.5 | async-start | bytes 6291456 | tf_op jit(solution)/shard_map/all_to_all | solution.py:310
  (4 other events, 7.8 us)
Sparse Core Ops, SparseCore 0:
  8.9 27.1 all-gather.2
  47.4 23.0 all-gather.4

commit v3 on v2

--- a/solution.py
+++ b/solution.py
@@ -314,6 +314,221 @@
     return jnp.sum(picked * gate_weights[:, :, None], axis=1)
 
 
+def route_kernel(capacity, marks_ref, info_ref, pick_ref, gate_ref):
+    planes, _, rows = info_ref.shape
+    row = lax.broadcasted_iota(jnp.int32, (rows, rows), 0)
+    col = lax.broadcasted_iota(jnp.int32, (rows, rows), 1)
+    before = (row < col).astype(jnp.bfloat16)
+    slot = lax.broadcasted_iota(jnp.int32, (capacity, rows), 0).astype(jnp.float32)
+    for block in range(planes):
+        for side in range(2):
+            mark = marks_ref[side].astype(jnp.float32)
+            named, gate = jnp.zeros((1, rows), jnp.float32), jnp.zeros((1, rows), jnp.float32)
+            for k in range(TOP):
+                hit = (info_ref[block, k : k + 1, :] == mark).astype(jnp.float32)
+                named = named + hit
+                gate = gate + hit * info_ref[block, TOP + k : TOP + k + 1, :]
+            wide = jnp.broadcast_to(named, (8, rows)).astype(jnp.bfloat16)
+            rank = jnp.dot(wide, before, preferred_element_type=jnp.float32)[0:1]
+            pick = jnp.where((slot == rank) & (named > 0.5), 1.0, 0.0)
+            pick_ref[block, side] = pick.astype(jnp.bfloat16)
+            gate_ref[block, :, side : side + 1] = jnp.sum(
+                jnp.where(row == col, gate, 0.0), axis=1, keepdims=True
+            )
+
+
+def compact_kernel(where_ref, pick_ref, *refs):
+    near_ref, far_ref = refs[-2:]
+    block = refs[0][...]
+    if len(refs) == 4:
+        block = jnp.where(where_ref[1] == 1, block, refs[1][...])
+    for side, out in enumerate((near_ref, far_ref)):
+        out[...] = jnp.dot(
+            pick_ref[where_ref[0], side], block, preferred_element_type=jnp.float32
+        ).astype(jnp.bfloat16)
+
+
+def expert_kernel(near_ref, far_ref, in_ref, out_ref, near_out, far_out, acc):
+    step = pl.program_id(0)
+    rows = jnp.concatenate([near_ref[...], far_ref[...]], axis=0)
+    pre = lax.dot_general(
+        rows, in_ref[...], (((1,), (1,)), ((), ())), preferred_element_type=jnp.float32
+    )
+    act = jax.nn.gelu(pre, approximate=True).astype(jnp.bfloat16)
+    part = jnp.dot(act, out_ref[...], preferred_element_type=jnp.float32)
+
+    @pl.when(step == 0)
+    def _():
+        acc[...] = part
+
+    @pl.when(step > 0)
+    def _():
+        acc[...] += part
+
+    @pl.when(step == pl.num_programs(0) - 1)
+    def _():
+        half = near_out.shape[0]
+        near_out[...] = acc[:half].astype(jnp.bfloat16)
+        far_out[...] = acc[half:].astype(jnp.bfloat16)
+
+
+def mixed_rows(block, pick_ref, gate_ref, outs):
+    total = 0.0
+    for side, out in enumerate(outs):
+        rows = lax.dot_general(
+            pick_ref[block, side],
+            out[...],
+            (((0,), (0,)), ((), ())),
+            preferred_element_type=jnp.float32,
+        )
+        total = total + gate_ref[block][:, side : side + 1] * rows
+    return total
+
+
+def combine_kernel(where_ref, pick_ref, gate_ref, near_ref, far_ref, out_ref):
+    out_ref[...] = mixed_rows(where_ref[0], pick_ref, gate_ref, (near_ref, far_ref)).astype(
+        jnp.bfloat16
+    )
+
+
+def final_kernel(
+    where_ref, pick_ref, gate_ref, near_ref, far_ref, residual_ref, mod_ref, *refs
+):
+    total = mixed_rows(where_ref[0], pick_ref, gate_ref, (near_ref, far_ref))
+    for ref in refs[:-1]:
+        total = total + ref[...].astype(jnp.float32)
+    refs[-1][...] = (residual_ref[...].astype(jnp.float32) + mod_ref[2:3, :] * total).astype(
+        jnp.bfloat16
+    )
+
+
+def small_call(kernel, shapes, flops, operands, scalars=1):
+    vmem = pl.BlockSpec(memory_space=pltpu.VMEM)
+    moved = sum(math.prod(o.shape) * o.dtype.itemsize for o in operands)
+    return pl.pallas_call(
+        kernel,
+        in_specs=[pl.BlockSpec(memory_space=pltpu.SMEM)] * scalars
+        + [vmem] * (len(operands) - scalars),
+        out_specs=[vmem] * len(shapes),
+        out_shape=shapes,
+        compiler_params=pltpu.CompilerParams(vmem_limit_bytes=VMEM_LIMIT),
+        cost_estimate=pl.CostEstimate(flops=flops, transcendentals=0, bytes_accessed=moved),
+    )(*operands)
+
+
+def passed_tokens_experts(
+    residual, normed, modulation, fc_in, fc_out, expert_ids, gate_weights
+):
+    planes, sides = lax.axis_size("seq"), lax.axis_size("expert")
+    plane, col = lax.axis_index("seq"), lax.axis_index("expert")
+    token_rows, width = normed.shape
+    capacity = 2 * TOP * token_rows // (planes * sides)
+    info = jnp.concatenate([expert_ids.T.astype(jnp.float32), gate_weights.T], axis=0)
+    info = lax.all_gather(info, "seq", axis=0, tiled=False)
+    marks = jnp.stack([plane * sides + col, plane * sides + 1 - col]).astype(jnp.int32)
+    pick, gate = small_call(
+        partial(route_kernel, capacity),
+        [
+            jax.ShapeDtypeStruct((planes, 2, capacity, token_rows), jnp.bfloat16),
+            jax.ShapeDtypeStruct((planes, token_rows, 2), jnp.float32),
+        ],
+        0,
+        (marks, info),
+    )
+    whole_in = lax.all_gather(fc_in, "fsdp", axis=1, tiled=True)[0]
+    whole_out = lax.all_gather(fc_out, "fsdp", axis=1, tiled=True)[0]
+    hidden = whole_in.shape[0]
+    chunk = min(256, hidden)
+    slots = jax.ShapeDtypeStruct((capacity, width), jnp.bfloat16)
+
+    def along(value, perm):
+        return lax.ppermute(value, "seq", perm)
+
+    def across(value, on):
+        perm = [(p * sides + x, p * sides + 1 - x) for p in on for x in range(sides)]
+        return lax.ppermute(value, ("seq", "expert"), perm)
+
+    def compact(where, blocks):
+        return small_call(
+            compact_kernel,
+            [slots, slots],
+            4 * capacity * token_rows * width,
+            (where, pick, *blocks),
+        )
+
+    def experts(near, far):
+        rows = pl.BlockSpec((capacity, width), lambda i: (0, 0))
+        weights = pl.BlockSpec((chunk, width), lambda i: (i, 0))
+        return pl.pallas_call(
+            expert_kernel,
+            grid=(hidden // chunk,),
+            in_specs=[rows, rows, weights, weights],
+            out_specs=[rows, rows],
+            out_shape=[slots, slots],
+            scratch_shapes=[pltpu.VMEM((2 * capacity, width), jnp.float32)],
+            compiler_params=pltpu.CompilerParams(vmem_limit_bytes=VMEM_LIMIT),
+            cost_estimate=pl.CostEstimate(
+                flops=8 * capacity * width * hidden,
+                transcendentals=2 * capacity * hidden,
+                bytes_accessed=4 * width * hidden,
+            ),
+            name="experts",
+        )(near, far, whole_in, whole_out)
+
+    def combine(where, near, far):
+        return small_call(
+            combine_kernel,
+            [jax.ShapeDtypeStruct((token_rows, width), jnp.bfloat16)],
+            4 * capacity * token_rows * width,
+            (where, pick, gate, near, far),
+        )[0]
+
+    last = planes - 1
+    left1 = along(normed, [(i, i + 1) for i in range(last)])
+    right1 = along(normed, [(i + 1, i) for i in range(last)])
+    left2 = along(left1, [(i, i + 1) for i in range(1, last)])
+    right2 = along(right1, [(i + 1, i) for i in range(last - 1)])
+    left3 = along(left2, [(2, 3)])
+    right3 = along(right2, [(1, 0)])
+
+    upper = (plane >= 2).astype(jnp.int32)
+
+    def where(block):
+        return jnp.stack([jnp.clip(block, 0, last), upper]).astype(jnp.int32)
+
+    stages = {
+        "own": (plane, (normed,), range(planes)),
+        "left": (plane - 1, (left1,), range(1, planes)),
+        "right": (plane + 1, (right1,), range(last)),
+        "two": (jnp.where(plane >= 2, plane - 2, plane + 2), (left2, right2), range(planes)),
+        "three": (last - plane, (left3, right3), (0, last)),
+    }
+    done = {}
+    for name, (block, blocks, on) in stages.items():
+        at = where(block)
+        near, far = compact(at, blocks)
+        came = across(far, on)
+        near_done, far_done = experts(near, came)
+        back = across(far_done, on)
+        done[name] = (at, near_done, back)
+    returned = []
+    for name, perm in (
+        ("left", [(i + 1, i) for i in range(last)]),
+        ("right", [(i, i + 1) for i in range(last)]),
+        ("two", [(0, 2), (1, 3), (2, 0), (3, 1)]),
+        ("three", [(0, last), (last, 0)]),
+    ):
+        summed = combine(*done[name])
+        returned.append(along(summed, perm))
+    at, near_done, back = done["own"]
+    return small_call(
+        final_kernel,
+        [jax.ShapeDtypeStruct((token_rows, width), jnp.bfloat16)],
+        4 * capacity * token_rows * width,
+        (at, pick, gate, near_done, back, residual, modulation, *returned),
+    )[0]
+
+
 def per_device(
     queries, keys, values, tokens, modulation, out_weight, fc_in, fc_out, expert_ids, gate_weights
 ):
@@ -327,6 +542,17 @@
     else:
         residual, normed = gathered_attention(
             queries, keys, values, tokens, modulation, out_weight
+        )
+    token_rows = tokens.shape[0]
+    capacity = 2 * TOP * token_rows // (fc_in.shape[0] * lax.axis_size(("seq", "expert")))
+    if (
+        planes == 4
+        and lax.axis_size("expert") == 2
+        and fc_in.shape[0] == 1
+        and 2 * capacity >= token_rows
+    ):
+        return passed_tokens_experts(
+            residual, normed, modulation, fc_in, fc_out, expert_ids, gate_weights
         )
     mixture = sent_tokens_experts(normed, fc_in, fc_out, expert_ids, gate_weights)
     return (residual.astype(jnp.float32) + modulation[2] * mixture).astype(jnp.bfloat16)

time: 353 us -> 405 us (1.15); the launches traced: 352 us -> 400 us
  Pallas kernels: 30.2 us -> 124 us
  waiting for transfers between devices: 222 us -> 152 us
  starting transfers between devices: 39.8 us -> 66.4 us
  blocking collectives: 0 us -> 25.2 us
  matrix products: 18.5 us -> 0 us
  local copies, waits for them, and re-layouts: 19.4 us -> 12.9 us
    all_to_all x2 -> x0, waiting for transfers between devices: 141 us -> none  [the longest x1 71.2 us: sent_tokens_experts(): lax.all_to_all(outgoing, ('seq', 'expert'), split_axis=0, concat_axis=0,...]
    pallas_call x0 -> x16, Pallas kernels: none -> 93.7 us  [the longest x5 64 us: experts(): pl.pallas_call(expert_kernel, grid=(hidden // chunk,), in_specs=[rows, ro...]
    ppermute x0 -> x20, waiting for transfers between devices: none -> 68.4 us  [the longest x10 62.2 us: along(): return lax.ppermute(value, 'seq', perm)]
    ppermute x0 -> x20, starting transfers between devices: none -> 35.7 us  [the longest x10 18.5 us: along(): return lax.ppermute(value, 'seq', perm)]
    all_gather x0 -> x1, blocking collectives: none -> 25.2 us  [passed_tokens_experts(): info = lax.all_gather(info, 'seq', axis=0, tiled=False)]
    dot_general x1 -> x0, matrix products: 18.5 us -> none  [expert_block(): jnp.dot(hidden_act.astype(jnp.bfloat16), weight_out, preferred_element_ty...]
    unnamed x28 -> x58, local copies, waits for them, and re-layouts: 1.73 us -> 10.1 us
    all_to_all x2 -> x0, starting transfers between devices: 8.1 us -> none  [the longest x1 4.06 us: sent_tokens_experts(): lax.all_to_all(outgoing, ('seq', 'expert'), split_axis=0, concat_axis=0,...]
  transfers between devices with their start and end apart: 23 -> 41, of which waited for: 11 -> 15; matrix products, arithmetic and copies ran while one was open for 4% -> 2% of each run, Pallas kernels for 9% -> 30%
where the time goes in v3:
time: 405 us; the launch traced here: 400 us
  waiting for transfers between devices  152 us (38%)
  Pallas kernels  124 us (31%)
  starting transfers between devices  66.4 us (16%)
  blocking collectives  25.2 us (6%)
  between operations  13.9 us (3%)
  local copies, waits for them, and re-layouts  12.9 us (3%)
  other arithmetic  5.8 us (1%)
    pallas_call x5, Pallas kernels, experts(): pl.pallas_call(expert_kernel, grid=(hidden // chunk,), in_specs=[rows, ro...  64 us
    ppermute x10, waiting for transfers between devices, along(): return lax.ppermute(value, 'seq', perm)  62.2 us
    ppermute x3, waiting for transfers between devices, moved_heads_attention(): from_x.append(swap('expert')(to_x[i * HEAD_DIM:(i + 1) * HEAD_DIM]))  47.3 us
    pallas_call x11, Pallas kernels, small_call(): pl.pallas_call(kernel, in_specs=[pl.BlockSpec(memory_space=pltpu.SMEM)] *...  29.7 us
    all_gather x1, blocking collectives, passed_tokens_experts(): info = lax.all_gather(info, 'seq', axis=0, tiled=False)  25.2 us
    all_to_all x1, waiting for transfers between devices, moved_heads_attention(): lax.all_to_all(second, 'seq', split_axis=0, concat_axis=0, tiled=True)  20.4 us
    ppermute x10, starting transfers between devices, along(): return lax.ppermute(value, 'seq', perm)  18.5 us
    ppermute x10, starting transfers between devices, across(): return lax.ppermute(value, ('seq', 'expert'), perm)  17.2 us
  transfers between devices with their start and end apart: 41, of which 15 were waited for; matrix products, arithmetic and copies ran while one was open for 2% of the time, Pallas kernels for 30%

profile of v3, /device:TPU:0, one launch (start us, length us, event | category | flops | bytes accessed | tf_op | source)
XLA Modules:
  0.0 399.5 jit_solution(18178749702843864730)
XLA Ops:
  8.0 3.4 pack.1
  15.6 6.2 %all-to-all-start.2 = ((bf16[4,3,256,128]{3,2,1,0:T(8,128)(2,1)}), bf16[4,3,256,128]{3,2,1,0:T(8,128)(2,1)S(1)}, u32[]{:S(2)}, u32[]{:S(2)}) async-start(bf16[4,3,256,128]{3,2,1,0:T(8,128)(2,1)} %maximum_select_fusion), calls=%async_computation.2 | async-start | bytes 1572864 | tf_op jit(solution)/shard_map/all_to_all | solution.py:171
  21.9 20.4 %all-to-all-done.2.query_ref.refs_0_.refs_1_ = bf16[4,3,256,128]{3,2,1,0:T(8,128)(2,1)S(1)} async-done(((bf16[4,3,256,128]{3,2,1,0:T(8,128)(2,1)}), bf16[4,3,256,128]{3,2,1,0:T(8,128)(2,1)S(1)}, u32[]{:S(2)}, u32[]{:S(2)}) %all-to-all-start.2) | async-done | bytes 786464 | tf_op jit(solution)/shard_map/all_to_all | solution.py:171
  42.3 3.6 all-to-all-start
  51.6 16.9 %collective-permute-done.3.refs_2_ = bf16[128,3072]{1,0:T(8,128)(2,1)S(1)} collective-permute-done((bf16[128,3072]{1,0:T(8,128)(2,1)S(1)}, bf16[128,3072]{1,0:T(8,128)(2,1)S(1)}, u32[]{:S(2)}, u32[]{:S(2)}) %collective-permute-start.3) | collective-permute-done | bytes 786464 | tf_op jit(solution)/shard_map/ppermute | solution.py:180
  70.0 15.4 %collective-permute-done.4.refs_3_ = bf16[128,3072]{1,0:T(8,128)(2,1)} collective-permute-done((bf16[128,3072]{1,0:T(8,128)(2,1)S(1)}, bf16[128,3072]{1,0:T(8,128)(2,1)}, u32[]{:S(2)}, u32[]{:S(2)}) %collective-permute-start.4) | collective-permute-done | bytes 786464 | tf_op jit(solution)/shard_map/ppermute | solution.py:180
  85.4 15.0 %collective-permute-done.5.refs_4_ = bf16[128,3072]{1,0:T(8,128)(2,1)} collective-permute-done((bf16[128,3072]{1,0:T(8,128)(2,1)S(1)}, bf16[128,3072]{1,0:T(8,128)(2,1)}, u32[]{:S(2)}, u32[]{:S(2)}) %collective-permute-start.5) | collective-permute-done | bytes 786464 | tf_op jit(solution)/shard_map/ppermute | solution.py:180
  103.7 6.2 %attention.3 = bf16[1024,128]{1,0:T(8,128)(2,1)} custom-call(bf16[4,3,256,128]{3,2,1,0:T(8,128)(2,1)} %copy-done, bf16[4,3,256,128]{3,2,1,0:T(8,128)(2,1)} %copy-done, bf16[4,3,256,128]{3,2,1,0:T(8,128)(2,1)} %copy-done, bf16[4,3,256,128]{3,2,1,0:T(8,128)(2,1)} %copy-done.1, bf16[4,3,256,128]{3,2,1,0:T(8,128)(2,1)} %copy-done.1), custom_call_target="tpu_custom_call" | custom-call | flops 1073741824 | bytes 1572864 | tf_op jit(solution)/shard_map/attention/pallas_call | solution.py:65
  109.9 6.2 %all-to-all-start.3 = ((bf16[16,64,128]{2,1,0:T(8,128)(2,1)}), bf16[16,64,128]{2,1,0:T(8,128)(2,1)S(1)}, u32[]{:S(2)}, u32[]{:S(2)}) async-start(bf16[16,64,128]{2,1,0:T(8,128)(2,1)} %bitcast.30), calls=%async_computation.3 | async-start | bytes 524288 | tf_op jit(solution)/shard_map/all_to_all | solution.py:196
  116.1 10.7 %attention.2 = bf16[2048,128]{1,0:T(8,128)(2,1)} custom-call(bf16[4,3,512,128]{3,2,1,0:T(8,128)(2,1)} %copy-done.3, bf16[4,3,512,128]{3,2,1,0:T(8,128)(2,1)} %copy-done.3, bf16[4,3,512,128]{3,2,1,0:T(8,128)(2,1)} %copy-done.3), custom_call_target="tpu_custom_call" | custom-call | flops 2147483648 | bytes 2097152 | tf_op jit(solution)/shard_map/attention/pallas_call | solution.py:65
  126.8 6.0 %all-to-all-start.1 = ((bf16[16,128,128]{2,1,0:T(8,128)(2,1)}), bf16[16,128,128]{2,1,0:T(8,128)(2,1)S(1)}, u32[]{:S(2)}, u32[]{:S(2)}) async-start(bf16[16,128,128]{2,1,0:T(8,128)(2,1)} %bitcast.31), calls=%async_computation.1 | async-start | bytes 1048576 | tf_op jit(solution)/shard_map/all_to_all | solution.py:188
  139.9 7.1 %all-to-all-done.1.full_ref = bf16[16,128,128]{2,1,0:T(8,128)(2,1)S(1)} async-done(((bf16[16,128,128]{2,1,0:T(8,128)(2,1)}), bf16[16,128,128]{2,1,0:T(8,128)(2,1)S(1)}, u32[]{:S(2)}, u32[]{:S(2)}) %all-to-all-start.1) | async-done | bytes 524320 | tf_op jit(solution)/shard_map/all_to_all | solution.py:188
  147.8 9.9 %project.1 = (bf16[128,3072]{1,0:T(8,128)(2,1)}, bf16[128,3072]{1,0:T(8,128)(2,1)}) custom-call(s32[24]{0:T(128)} %concatenate.13.slots_ref, bf16[16,128,128]{2,1,0:T(8,128)(2,1)} %copy-done.2, bf16[8,128,128]{2,1,0:T(8,128)(2,1)} %bitcast.29, bf16[128,3072]{1,0:T(8,128)(2,1)} %tokens_ref.1, f32[3,3072]{1,0:T(4,128)} %mod_ref.3, bf16[768,3072]{1,0:T(8,128)(2,1)} %refs_0_.1, ...), custom_call_target="tpu_custom_call" | custom-call | flops 2415919104 | bytes 18874368 | tf_op jit(solution)/shard_map/project/pallas_call | solution.py:229
  157.7 3.1 collective-permute-start.17
  162.1 16.7 %collective-permute-done.17.refs_0_ = bf16[128,3072]{1,0:T(8,128)(2,1)S(1)} collective-permute-done((bf16[128,3072]{1,0:T(8,128)(2,1)}, bf16[128,3072]{1,0:T(8,128)(2,1)S(1)}, u32[]{:S(2)}, u32[]{:S(2)}) %collective-permute-start.17) | collective-permute-done | bytes 786464 | tf_op jit(solution)/shard_map/ppermute | solution.py:445
  179.5 3.3 collective-permute-done.21.refs_0_
  184.9 18.9 %collective-permute-done.26.refs_1_ = bf16[128,3072]{1,0:T(8,128)(2,1)S(1)} collective-permute-done((bf16[128,3072]{1,0:T(8,128)(2,1)S(1)}, bf16[128,3072]{1,0:T(8,128)(2,1)S(1)}, u32[]{:S(2)}, u32[]{:S(2)}) %collective-permute-start.26) | collective-permute-done | bytes 786464 | tf_op jit(solution)/shard_map/ppermute | solution.py:445
  205.1 25.2 %all-gather.1.info_ref = f32[4,4,128]{2,1,0:T(4,128)} all-gather(f32[1,4,128]{2,1,0:T(4,128)S(1)} %maximum_bitcast_fusion), channel_id=2, replica_groups=mesh['group'=2,'seq'=4,'expert'=2,'fsdp'=2] {'seq'}, dimensions={0}, use_global_device_ids=true | all-gather | bytes 10240 | tf_op jit(solution)/shard_map/all_gather | solution.py:427
  254.4 12.8 %experts.6 = (bf16[64,3072]{1,0:T(8,128)(2,1)}, bf16[64,3072]{1,0:T(8,128)(2,1)}) custom-call(bf16[64,3072]{1,0:T(8,128)(2,1)} %get-tuple-element.43.near_ref, bf16[64,3072]{1,0:T(8,128)(2,1)} %copy-done.24, bf16[1536,3072]{1,0:T(8,128)(2,1)} %bitcast.19, bf16[1536,3072]{1,0:T(8,128)(2,1)} %bitcast.24), custom_call_target="tpu_custom_call" | custom-call | flops 2415919104 | bytes 18874368 | tf_op jit(solution)/shard_map/experts/pallas_call | solution.py:462
  267.9 12.8 %experts.7 = (bf16[64,3072]{1,0:T(8,128)(2,1)}, bf16[64,3072]{1,0:T(8,128)(2,1)}) custom-call(bf16[64,3072]{1,0:T(8,128)(2,1)} %get-tuple-element.47.near_ref, bf16[64,3072]{1,0:T(8,128)(2,1)} %collective-permute-done.22.far_ref, bf16[1536,3072]{1,0:T(8,128)(2,1)} %bitcast.20, bf16[1536,3072]{1,0:T(8,128)(2,1)} %bitcast.25), custom_call_target="tpu_custom_call" | custom-call | flops 2415919104 | bytes 18874368 | tf_op jit(solution)/shard_map/experts/pallas_call | solution.py:462
  280.7 3.7 collective-permute-start.23
  284.4 12.8 %experts.8 = (bf16[64,3072]{1,0:T(8,128)(2,1)}, bf16[64,3072]{1,0:T(8,128)(2,1)}) custom-call(bf16[64,3072]{1,0:T(8,128)(2,1)} %get-tuple-element.51.near_ref, bf16[64,3072]{1,0:T(8,128)(2,1)} %collective-permute-done.27.far_ref, bf16[1536,3072]{1,0:T(8,128)(2,1)} %bitcast.21, bf16[1536,3072]{1,0:T(8,128)(2,1)} %bitcast.26), custom_call_target="tpu_custom_call" | custom-call | flops 2415919104 | bytes 18874368 | tf_op jit(solution)/shard_map/experts/pallas_call | solution.py:462
  298.2 12.8 %experts.9 = (bf16[64,3072]{1,0:T(8,128)(2,1)}, bf16[64,3072]{1,0:T(8,128)(2,1)}) custom-call(bf16[64,3072]{1,0:T(8,128)(2,1)} %get-tuple-element.55.near_ref, bf16[64,3072]{1,0:T(8,128)(2,1)} %copy-done.26, bf16[1536,3072]{1,0:T(8,128)(2,1)} %bitcast.22, bf16[1536,3072]{1,0:T(8,128)(2,1)} %bitcast.27), custom_call_target="tpu_custom_call" | custom-call | flops 2415919104 | bytes 18874368 | tf_op jit(solution)/shard_map/experts/pallas_call | solution.py:462
  311.0 3.7 collective-permute-start.33
  326.2 4.6 %collective-permute-start.24 = (bf16[128,3072]{1,0:T(8,128)(2,1)}, bf16[128,3072]{1,0:T(8,128)(2,1)S(1)}, u32[]{:S(2)}, u32[]{:S(2)}) collective-permute-start(bf16[128,3072]{1,0:T(8,128)(2,1)} %shard_map.105), channel_id=1, source_target_pairs={{0,4},{4,8},{8,12},{1,5},{5,9},{9,13},{2,6},{6,10},{10,14},{3,7},{... | collective-permute-start | bytes 2359304 | tf_op jit(solution)/shard_map/ppermute | solution.py:445
  331.6 2.8 shard_map.107
  336.2 2.8 shard_map.109
  339.0 3.2 collective-permute-start.34
  342.9 12.8 %experts.5 = (bf16[64,3072]{1,0:T(8,128)(2,1)}, bf16[64,3072]{1,0:T(8,128)(2,1)}) custom-call(bf16[64,3072]{1,0:T(8,128)(2,1)} %get-tuple-element.38.near_ref, bf16[64,3072]{1,0:T(8,128)(2,1)} %copy-done.25, bf16[1536,3072]{1,0:T(8,128)(2,1)} %bitcast.23, bf16[1536,3072]{1,0:T(8,128)(2,1)} %bitcast.28), custom_call_target="tpu_custom_call" | custom-call | flops 2415919104 | bytes 18874368 | tf_op jit(solution)/shard_map/experts/pallas_call | solution.py:462
  357.5 6.2 %collective-permute-done.16.far_ref = bf16[64,3072]{1,0:T(8,128)(2,1)S(1)} collective-permute-done((bf16[64,3072]{1,0:T(8,128)(2,1)}, bf16[64,3072]{1,0:T(8,128)(2,1)S(1)}, u32[]{:S(2)}, u32[]{:S(2)}) %collective-permute-start.16) | collective-permute-done | bytes 393248 | tf_op jit(solution)/shard_map/ppermute | solution.py:449
  363.7 23.2 %collective-permute-done.29.refs_2_ = bf16[128,3072]{1,0:T(8,128)(2,1)S(1)} collective-permute-done((bf16[128,3072]{1,0:T(8,128)(2,1)}, bf16[128,3072]{1,0:T(8,128)(2,1)S(1)}, u32[]{:S(2)}, u32[]{:S(2)}) %collective-permute-start.29) | collective-permute-done | bytes 786464 | tf_op jit(solution)/shard_map/ppermute | solution.py:445
  388.1 4.6 %shard_map.110 = bf16[128,3072]{1,0:T(8,128)(2,1)} custom-call(s32[2]{0:T(128)} %pad_add_fusion.where_ref, bf16[4,2,64,128]{3,2,1,0:T(8,128)(2,1)} %get-tuple-element.32.pick_ref, f32[4,128,2]{2,1,0:T(8,128)} %get-tuple-element.33.gate_ref, bf16[64,3072]{1,0:T(8,128)(2,1)} %get-tuple-element.40.near_ref, bf16[64,3072]{1,0:T(8,128)(2,1)} %copy-done.19, ...), custom_call_target="tpu_custom_call" | custom-call | flops 100663296 | bytes 4890632 | tf_op jit(solution)/shard_map/pallas_call | solution.py:408
  (145 shorter events, 72.8 us)
Async XLA Ops:
  6.5 247.1 %all-gather.5.cloned.1.call-start = ((), (), s32[]{:S(2)}) async-start(), calls=%async_computation.4 | async-start | bytes 14155776 | tf_op jit(solution)/shard_map/all_gather | solution.py:438
  7.3 246.4 %all-gather.7.cloned.1.call-start = ((), (), s32[]{:S(2)}) async-start(), calls=%async_computation.5 | async-start | bytes 14155776 | tf_op jit(solution)/shard_map/all_gather | solution.py:439
  15.6 26.6 %all-to-all-start.2 = ((bf16[4,3,256,128]{3,2,1,0:T(8,128)(2,1)}), bf16[4,3,256,128]{3,2,1,0:T(8,128)(2,1)S(1)}, u32[]{:S(2)}, u32[]{:S(2)}) async-start(bf16[4,3,256,128]{3,2,1,0:T(8,128)(2,1)} %maximum_select_fusion), calls=%async_computation.2 | async-start | bytes 1572864 | tf_op jit(solution)/shard_map/all_to_all | solution.py:171
  21.9 125.2 %collective-permute-start.2 = (bf16[768,3072]{1,0:T(8,128)(2,1)}, bf16[768,3072]{1,0:T(8,128)(2,1)}, u32[]{:S(2)}, u32[]{:S(2)}) collective-permute-start(bf16[768,3072]{1,0:T(8,128)(2,1)} %refs_0_.1), channel_id=1, source_target_pairs={{0,1},{1,0},{2,3},{3,2},{4,5},{5,4},{6,7},{7,6},{8,9},{9,8},{10,11... | collective-permute-start | bytes 14155784 | tf_op jit(solution)/shard_map/ppermute | solution.py:177
  42.3 67.6 %all-to-all-start = ((bf16[4,3,512,128]{3,2,1,0:T(8,128)(2,1)}), bf16[4,3,512,128]{3,2,1,0:T(8,128)(2,1)S(1)}, u32[]{:S(2)}, u32[]{:S(2)}) async-start(bf16[4,3,512,128]{3,2,1,0:T(8,128)(2,1)} %get-tuple-element.34), calls=%async_computation | async-start | bytes 3145728 | tf_op jit(solution)/shard_map/all_to_all | solution.py:166
  48.0 20.5 %collective-permute-start.3 = (bf16[128,3072]{1,0:T(8,128)(2,1)S(1)}, bf16[128,3072]{1,0:T(8,128)(2,1)S(1)}, u32[]{:S(2)}, u32[]{:S(2)}) collective-permute-start(bf16[128,3072]{1,0:T(8,128)(2,1)S(1)} %get-tuple-element.61), channel_id=1, source_target_pairs={{0,2},{2,0},{1,3},{3,1},{4,6},{6,4},{5,7},{7,5},{8,10},{10,8},{9,1... | collective-permute-start | bytes 2359304 | tf_op jit(solution)/shard_map/ppermute | solution.py:180
  49.6 35.9 %collective-permute-start.4 = (bf16[128,3072]{1,0:T(8,128)(2,1)S(1)}, bf16[128,3072]{1,0:T(8,128)(2,1)}, u32[]{:S(2)}, u32[]{:S(2)}) collective-permute-start(bf16[128,3072]{1,0:T(8,128)(2,1)S(1)} %get-tuple-element.60), channel_id=1, source_target_pairs={{0,2},{2,0},{1,3},{3,1},{4,6},{6,4},{5,7},{7,5},{8,10},{10,8},{9,1... | collective-permute-start | bytes 2359304 | tf_op jit(solution)/shard_map/ppermute | solution.py:180
  50.1 50.3 %collective-permute-start.5 = (bf16[128,3072]{1,0:T(8,128)(2,1)S(1)}, bf16[128,3072]{1,0:T(8,128)(2,1)}, u32[]{:S(2)}, u32[]{:S(2)}) collective-permute-start(bf16[128,3072]{1,0:T(8,128)(2,1)S(1)} %get-tuple-element.59), channel_id=1, source_target_pairs={{0,2},{2,0},{1,3},{3,1},{4,6},{6,4},{5,7},{7,5},{8,10},{10,8},{9,1... | collective-permute-start | bytes 2359304 | tf_op jit(solution)/shard_map/ppermute | solution.py:180
  68.5 33.3 %collective-permute-start.6 = (bf16[128,3072]{1,0:T(8,128)(2,1)S(1)}, bf16[128,3072]{1,0:T(8,128)(2,1)S(1)}, u32[]{:S(2)}, u32[]{:S(2)}) collective-permute-start(bf16[128,3072]{1,0:T(8,128)(2,1)S(1)} %collective-permute-done.3.refs_2_), channel_id=1, source_target_pairs={{0,16},{16,0},{1,17},{17,1},{2,18},{18,2},{3,19},{19,3},{4,20},{20... | collective-permute-start | bytes 2359304 | tf_op jit(solution)/shard_map/ppermute | solution.py:182
  70.0 31.8 %collective-permute-start.1 = (bf16[4,3,256,128]{3,2,1,0:T(8,128)(2,1)S(1)}, bf16[4,3,256,128]{3,2,1,0:T(8,128)(2,1)S(1)}, u32[]{:S(2)}, u32[]{:S(2)}) collective-permute-start(bf16[4,3,256,128]{3,2,1,0:T(8,128)(2,1)S(1)} %all-to-all-done.2.query_ref.refs_0_.refs_1_), channel_id=1, source_target_pairs={{0,1},{1,0},{2,3},{3,2},{4,5},{5,4},{6,7},{7,6},{8,9},{9,8},{10,11... | collective-permute-start | bytes 2359304 | tf_op jit(solution)/shard_map/ppermute | solution.py:172
  85.4 49.8 %collective-permute-start.9 = (bf16[128,3072]{1,0:T(8,128)(2,1)S(1)}, bf16[128,3072]{1,0:T(8,128)(2,1)}, u32[]{:S(2)}, u32[]{:S(2)}) collective-permute-start(bf16[128,3072]{1,0:T(8,128)(2,1)S(1)} %collective-permute-done.3.refs_2_), channel_id=1, source_target_pairs={{0,1},{1,0},{2,3},{3,2},{4,5},{5,4},{6,7},{7,6},{8,9},{9,8},{10,11... | collective-permute-start | bytes 2359304 | tf_op jit(solution)/shard_map/ppermute | solution.py:184
  100.4 32.4 %collective-permute-start.7 = (bf16[128,3072]{1,0:T(8,128)(2,1)}, bf16[128,3072]{1,0:T(8,128)(2,1)}, u32[]{:S(2)}, u32[]{:S(2)}) collective-permute-start(bf16[128,3072]{1,0:T(8,128)(2,1)} %collective-permute-done.4.refs_3_), channel_id=1, source_target_pairs={{0,16},{16,0},{1,17},{17,1},{2,18},{18,2},{3,19},{19,3},{4,20},{20... | collective-permute-start | bytes 2359304 | tf_op jit(solution)/shard_map/ppermute | solution.py:182
  101.8 33.9 %collective-permute-start.10 = (bf16[128,3072]{1,0:T(8,128)(2,1)}, bf16[128,3072]{1,0:T(8,128)(2,1)}, u32[]{:S(2)}, u32[]{:S(2)}) collective-permute-start(bf16[128,3072]{1,0:T(8,128)(2,1)} %collective-permute-done.4.refs_3_), channel_id=1, source_target_pairs={{0,1},{1,0},{2,3},{3,2},{4,5},{5,4},{6,7},{7,6},{8,9},{9,8},{10,11... | collective-permute-start | bytes 2359304 | tf_op jit(solution)/shard_map/ppermute | solution.py:184
  102.7 32.5 %collective-permute-start.8 = (bf16[128,3072]{1,0:T(8,128)(2,1)}, bf16[128,3072]{1,0:T(8,128)(2,1)}, u32[]{:S(2)}, u32[]{:S(2)}) collective-permute-start(bf16[128,3072]{1,0:T(8,128)(2,1)} %collective-permute-done.5.refs_4_), channel_id=1, source_target_pairs={{0,16},{16,0},{1,17},{17,1},{2,18},{18,2},{3,19},{19,3},{4,20},{20... | collective-permute-start | bytes 2359304 | tf_op jit(solution)/shard_map/ppermute | solution.py:182
  126.8 20.3 %all-to-all-start.1 = ((bf16[16,128,128]{2,1,0:T(8,128)(2,1)}), bf16[16,128,128]{2,1,0:T(8,128)(2,1)S(1)}, u32[]{:S(2)}, u32[]{:S(2)}) async-start(bf16[16,128,128]{2,1,0:T(8,128)(2,1)} %bitcast.31), calls=%async_computation.1 | async-start | bytes 1048576 | tf_op jit(solution)/shard_map/all_to_all | solution.py:188
  157.7 21.1 %collective-permute-start.17 = (bf16[128,3072]{1,0:T(8,128)(2,1)}, bf16[128,3072]{1,0:T(8,128)(2,1)S(1)}, u32[]{:S(2)}, u32[]{:S(2)}) collective-permute-start(bf16[128,3072]{1,0:T(8,128)(2,1)} %get-tuple-element.37.refs_0_), channel_id=1, source_target_pairs={{0,4},{4,8},{8,12},{1,5},{5,9},{9,13},{2,6},{6,10},{10,14},{3,7},{... | collective-permute-start | bytes 2359304 | tf_op jit(solution)/shard_map/ppermute | solution.py:445
  160.8 22.0 %collective-permute-start.21 = (bf16[128,3072]{1,0:T(8,128)(2,1)}, bf16[128,3072]{1,0:T(8,128)(2,1)S(1)}, u32[]{:S(2)}, u32[]{:S(2)}) collective-permute-start(bf16[128,3072]{1,0:T(8,128)(2,1)} %get-tuple-element.37.refs_0_), channel_id=1, source_target_pairs={{4,0},{8,4},{12,8},{5,1},{9,5},{13,9},{6,2},{10,6},{14,10},{7,3},{... | collective-permute-start | bytes 2359304 | tf_op jit(solution)/shard_map/ppermute | solution.py:445
  182.8 20.9 %collective-permute-start.26 = (bf16[128,3072]{1,0:T(8,128)(2,1)S(1)}, bf16[128,3072]{1,0:T(8,128)(2,1)S(1)}, u32[]{:S(2)}, u32[]{:S(2)}) collective-permute-start(bf16[128,3072]{1,0:T(8,128)(2,1)S(1)} %collective-permute-done.21.refs_0_), channel_id=1, source_target_pairs={{4,0},{8,4},{5,1},{9,5},{6,2},{10,6},{7,3},{11,7},{20,16},{24,20},... | collective-permute-start | bytes 2359304 | tf_op jit(solution)/shard_map/ppermute | solution.py:445
  184.1 62.9 %collective-permute-start.30 = (bf16[128,3072]{1,0:T(8,128)(2,1)S(1)}, bf16[128,3072]{1,0:T(8,128)(2,1)S(1)}, u32[]{:S(2)}, u32[]{:S(2)}) collective-permute-start(bf16[128,3072]{1,0:T(8,128)(2,1)S(1)} %collective-permute-done.25.refs_0_), channel_id=1, source_target_pairs={{8,12},{9,13},{10,14},{11,15},{24,28},{25,29},{26,30},{27,31}} | collective-permute-start | bytes 2359304 | tf_op jit(solution)/shard_map/ppermute | solution.py:445
  203.8 43.2 %collective-permute-start.31 = (bf16[128,3072]{1,0:T(8,128)(2,1)S(1)}, bf16[128,3072]{1,0:T(8,128)(2,1)S(1)}, u32[]{:S(2)}, u32[]{:S(2)}) collective-permute-start(bf16[128,3072]{1,0:T(8,128)(2,1)S(1)} %collective-permute-done.26.refs_1_), channel_id=1, source_target_pairs={{4,0},{5,1},{6,2},{7,3},{20,16},{21,17},{22,18},{23,19}} | collective-permute-start | bytes 2359304 | tf_op jit(solution)/shard_map/ppermute | solution.py:445
  239.2 28.6 %collective-permute-start.22 = (bf16[64,3072]{1,0:T(8,128)(2,1)}, bf16[64,3072]{1,0:T(8,128)(2,1)}, u32[]{:S(2)}, u32[]{:S(2)}) collective-permute-start(bf16[64,3072]{1,0:T(8,128)(2,1)} %get-tuple-element.48), channel_id=1, source_target_pairs={{0,2},{2,0},{4,6},{6,4},{8,10},{10,8},{1,3},{3,1},{5,7},{7,5},{9,1... | collective-permute-start | bytes 1179656 | tf_op jit(solution)/shard_map/ppermute | solution.py:449
  245.2 39.2 %collective-permute-start.27 = (bf16[64,3072]{1,0:T(8,128)(2,1)}, bf16[64,3072]{1,0:T(8,128)(2,1)}, u32[]{:S(2)}, u32[]{:S(2)}) collective-permute-start(bf16[64,3072]{1,0:T(8,128)(2,1)} %get-tuple-element.52), channel_id=1, source_target_pairs={{0,2},{2,0},{4,6},{6,4},{8,10},{10,8},{12,14},{14,12},{1,3},{3,1},... | collective-permute-start | bytes 1179656 | tf_op jit(solution)/shard_map/ppermute | solution.py:449
  251.4 46.1 %collective-permute-start.32 = (bf16[64,3072]{1,0:T(8,128)(2,1)}, bf16[64,3072]{1,0:T(8,128)(2,1)S(1)}, u32[]{:S(2)}, u32[]{:S(2)}) collective-permute-start(bf16[64,3072]{1,0:T(8,128)(2,1)} %get-tuple-element.56), channel_id=1, source_target_pairs={{0,2},{2,0},{12,14},{14,12},{1,3},{3,1},{13,15},{15,13},{16,18},{1... | collective-permute-start | bytes 1179656 | tf_op jit(solution)/shard_map/ppermute | solution.py:449
  267.2 50.8 %collective-permute-start.19 = (bf16[64,3072]{1,0:T(8,128)(2,1)}, bf16[64,3072]{1,0:T(8,128)(2,1)S(1)}, u32[]{:S(2)}, u32[]{:S(2)}) collective-permute-start(bf16[64,3072]{1,0:T(8,128)(2,1)} %get-tuple-element.46), channel_id=1, source_target_pairs={{4,6},{6,4},{8,10},{10,8},{12,14},{14,12},{5,7},{7,5},{9,11},{11,9... | collective-permute-start | bytes 1179656 | tf_op jit(solution)/shard_map/ppermute | solution.py:449
  280.7 42.1 %collective-permute-start.23 = (bf16[64,3072]{1,0:T(8,128)(2,1)}, bf16[64,3072]{1,0:T(8,128)(2,1)S(1)}, u32[]{:S(2)}, u32[]{:S(2)}) collective-permute-start(bf16[64,3072]{1,0:T(8,128)(2,1)} %get-tuple-element.50), channel_id=1, source_target_pairs={{0,2},{2,0},{4,6},{6,4},{8,10},{10,8},{1,3},{3,1},{5,7},{7,5},{9,1... | collective-permute-start | bytes 1179656 | tf_op jit(solution)/shard_map/ppermute | solution.py:449
  297.2 33.6 %collective-permute-start.28 = (bf16[64,3072]{1,0:T(8,128)(2,1)}, bf16[64,3072]{1,0:T(8,128)(2,1)S(1)}, u32[]{:S(2)}, u32[]{:S(2)}) collective-permute-start(bf16[64,3072]{1,0:T(8,128)(2,1)} %get-tuple-element.54), channel_id=1, source_target_pairs={{0,2},{2,0},{4,6},{6,4},{8,10},{10,8},{12,14},{14,12},{1,3},{3,1},... | collective-permute-start | bytes 1179656 | tf_op jit(solution)/shard_map/ppermute | solution.py:449
  311.0 24.5 %collective-permute-start.33 = (bf16[64,3072]{1,0:T(8,128)(2,1)}, bf16[64,3072]{1,0:T(8,128)(2,1)S(1)}, u32[]{:S(2)}, u32[]{:S(2)}) collective-permute-start(bf16[64,3072]{1,0:T(8,128)(2,1)} %get-tuple-element.58), channel_id=1, source_target_pairs={{0,2},{2,0},{12,14},{14,12},{1,3},{3,1},{13,15},{15,13},{16,18},{1... | collective-permute-start | bytes 1179656 | tf_op jit(solution)/shard_map/ppermute | solution.py:449
  317.8 24.4 %collective-permute-start.15 = (bf16[64,3072]{1,0:T(8,128)(2,1)}, bf16[64,3072]{1,0:T(8,128)(2,1)S(1)}, u32[]{:S(2)}, u32[]{:S(2)}) collective-permute-start(bf16[64,3072]{1,0:T(8,128)(2,1)} %get-tuple-element.39), channel_id=1, source_target_pairs={{0,2},{2,0},{4,6},{6,4},{8,10},{10,8},{12,14},{14,12},{1,3},{3,1},... | collective-permute-start | bytes 1179656 | tf_op jit(solution)/shard_map/ppermute | solution.py:449
  321.4 42.3 %collective-permute-start.20 = (bf16[128,3072]{1,0:T(8,128)(2,1)}, bf16[128,3072]{1,0:T(8,128)(2,1)S(1)}, u32[]{:S(2)}, u32[]{:S(2)}) collective-permute-start(bf16[128,3072]{1,0:T(8,128)(2,1)} %shard_map.103), channel_id=1, source_target_pairs={{4,0},{8,4},{12,8},{5,1},{9,5},{13,9},{6,2},{10,6},{14,10},{7,3},{... | collective-permute-start | bytes 2359304 | tf_op jit(solution)/shard_map/ppermute | solution.py:445
  326.2 37.5 %collective-permute-start.24 = (bf16[128,3072]{1,0:T(8,128)(2,1)}, bf16[128,3072]{1,0:T(8,128)(2,1)S(1)}, u32[]{:S(2)}, u32[]{:S(2)}) collective-permute-start(bf16[128,3072]{1,0:T(8,128)(2,1)} %shard_map.105), channel_id=1, source_target_pairs={{0,4},{4,8},{8,12},{1,5},{5,9},{9,13},{2,6},{6,10},{10,14},{3,7},{... | collective-permute-start | bytes 2359304 | tf_op jit(solution)/shard_map/ppermute | solution.py:445
  334.4 52.6 %collective-permute-start.29 = (bf16[128,3072]{1,0:T(8,128)(2,1)}, bf16[128,3072]{1,0:T(8,128)(2,1)S(1)}, u32[]{:S(2)}, u32[]{:S(2)}) collective-permute-start(bf16[128,3072]{1,0:T(8,128)(2,1)} %shard_map.107), channel_id=1, source_target_pairs={{0,8},{4,12},{8,0},{12,4},{1,9},{5,13},{9,1},{13,5},{2,10},{6,14},... | collective-permute-start | bytes 2359304 | tf_op jit(solution)/shard_map/ppermute | solution.py:445
  339.0 48.0 %collective-permute-start.34 = (bf16[128,3072]{1,0:T(8,128)(2,1)}, bf16[128,3072]{1,0:T(8,128)(2,1)S(1)}, u32[]{:S(2)}, u32[]{:S(2)}) collective-permute-start(bf16[128,3072]{1,0:T(8,128)(2,1)} %shard_map.109), channel_id=1, source_target_pairs={{0,12},{12,0},{1,13},{13,1},{2,14},{14,2},{3,15},{15,3},{16,28},{2... | collective-permute-start | bytes 2359304 | tf_op jit(solution)/shard_map/ppermute | solution.py:445
  (38 other events, 605.4 us)
Sparse Core Ops, SparseCore 0:
  8.9 27.9 all-gather.4
  38.4 23.0 all-gather.6
